TPU v7x, 256 devices: a whole 4x4x8 slice. The times are simulated.
256 devices in a mesh: seq: 32 (over x, z), head: 8 (over y, core).
Axes of the slice: x: 4, y: 4, z: 8, core: 2. Of those that a mesh axis runs over, the one named last changes fastest.
Arguments:
- hidden_in: bfloat16 [8192, 2048], P('seq'), may hold values from -6 to 6
- w_qk: bfloat16 [2048, 2, 2048], P(None, None, 'head'), may hold values from -0.125 to 0.125
- w_value: bfloat16 [2048, 4096], P(None, 'head'), may hold values from -0.125 to 0.125
- w_outgate: bfloat16 [2048, 4096], P(None, 'head'), may hold values from -0.125 to 0.125
- w_ba: bfloat16 [2048, 2, 32], P(None, None, 'head'), may hold values from -0.125 to 0.125
- conv_qk: bfloat16 [4, 2, 2048], P(None, None, 'head'), may hold values from -3 to 3
- conv_value: bfloat16 [4, 4096], P(None, 'head'), may hold values from -3 to 3
- hist_qk: bfloat16 [3, 2, 2048], P(None, None, 'head'), may hold values from -6 to 6
- hist_value: bfloat16 [3, 4096], P(None, 'head'), may hold values from -6 to 6
- a_log: float32 [32], P('head'), may hold values from -11 to -3
- dt_bias: float32 [32], P('head'), may hold values from -1 to 1
- beta_bias: float32 [32], P('head'), may hold values from -1 to 1
- state_in: float32 [32, 128, 128], P('head'), may hold values from -0.6 to 0.6
- norm_gain: float32 [128], replicated, may hold values from 0.5 to 1.5
- w_out: bfloat16 [4096, 2048], P('head'), may hold values from -0.09375 to 0.09375
Outputs:
- mixed: bfloat16 [8192, 2048], P('seq', 'head')
- checkpoints: float32 [32, 32, 128, 128], P('seq', 'head')
All inputs are finite; a program needn't handle non-finite values.
Results may differ from a plain program's by a relative error of at most 0.015.
Values may be sent and summed in bfloat16 or wider, within the bound.
A program may use at most 64 MiB of HBM per device.

v0:
```python
import jax
import jax.numpy as jnp
from jax import lax
from jax.sharding import PartitionSpec as P

KEY_HEAD_SIZE = 128
DV = 128
SPAN = 64


exact_setting = lax.Precision.HIGHEST


def shifted(value, axis, steps):
    count = lax.axis_size(axis)
    leading, last = (max(0, -steps), min(count, count - steps))
    return lax.ppermute(value, axis, [(source, source + steps) for source in range(leading, last)])


def entering(value, axis, join, neutral):
    place = lax.axis_index(axis)
    gathered = jax.tree.map(
        lambda a, kind: lax.all_gather(a.astype(kind), axis), value, (jnp.bfloat16, jnp.bfloat16)
    )
    state = jax.tree.map(lambda a, e: jnp.zeros_like(a) + jnp.asarray(e, a.dtype), value, neutral)

    def one(turn, state):
        return join(
            state,
            jax.tree.map(
                lambda a, own: lax.dynamic_index_in_dim(a, turn, 0, False).astype(own.dtype),
                gathered,
                value,
            ),
        )

    return lax.fori_loop(0, place, one, state)


def stored(values):
    return lax.optimization_barrier(values.astype(jnp.bfloat16))


def unit_rows(values):
    return values * lax.rsqrt(jnp.sum(values * values, axis=-1, keepdims=True) + 1e-06)


def causal_filter(history, present, weight):
    joined = jnp.concatenate([history, present], 0).astype(jnp.float32)
    count = present.shape[0]
    total = jnp.zeros(present.shape, jnp.float32)
    for offset in range(weight.shape[0]):
        total = total + weight[offset].astype(jnp.float32) * joined[offset : offset + count]
    return jax.nn.silu(total)


def mat_batch(left, right):
    return jnp.einsum("hij,hjk->hik", left, right, precision=exact_setting)


def to_front(values):
    return jnp.moveaxis(values, 1, 0)


def local(
    hidden_in,
    w_qk,
    w_value,
    w_outgate,
    w_ba,
    conv_qk,
    conv_value,
    hist_qk,
    hist_value,
    a_log,
    dt_bias,
    beta_bias,
    state_in,
    norm_gain,
    w_out,
):
    num_rows, model_width = hidden_in.shape
    key_cols = w_qk.shape[2]
    heads = a_log.shape[0]
    key_heads = key_cols // KEY_HEAD_SIZE
    taps = conv_value.shape[0]
    qk_flat = w_qk.reshape(model_width, 2 * key_cols)
    pre_qk = stored(jnp.dot(hidden_in, qk_flat, preferred_element_type=jnp.float32))
    pre_value = stored(jnp.dot(hidden_in, w_value, preferred_element_type=jnp.float32))
    rim_start = num_rows - (taps - 1)
    packed = jnp.concatenate([pre_qk[rim_start:], pre_value[rim_start:]], 1)
    moved = shifted(packed, "seq", 1)
    prev_qk = moved[:, : 2 * key_cols]
    prev_value = moved[:, 2 * key_cols :]
    leading = lax.axis_index("seq") == 0
    prev_qk = jnp.where(leading, hist_qk.reshape(taps - 1, 2 * key_cols), prev_qk)
    prev_value = jnp.where(leading, hist_value, prev_value)
    mixed_qk = causal_filter(prev_qk, pre_qk, conv_qk.reshape(taps, 2 * key_cols)).reshape(
        num_rows, 2, key_heads, KEY_HEAD_SIZE
    )
    values = causal_filter(prev_value, pre_value, conv_value).reshape(num_rows, heads, DV)
    ratio = heads // key_heads
    queries = jnp.repeat(unit_rows(mixed_qk[:, 0]) * KEY_HEAD_SIZE ** (-0.5), ratio, axis=1)
    keys = jnp.repeat(unit_rows(mixed_qk[:, 1]), ratio, axis=1)
    gates_in = (
        stored(
            jnp.dot(
                hidden_in, w_ba.reshape(model_width, 2 * heads), preferred_element_type=jnp.float32
            )
        )
        .astype(jnp.float32)
        .reshape(num_rows, 2, heads)
    )
    strength = jax.nn.sigmoid(gates_in[:, 0] + beta_bias)
    log_decay = -jnp.exp(a_log) * jax.nn.softplus(gates_in[:, 1] + dt_bias)
    blocks = num_rows // SPAN

    def spanned(values_in):
        return jnp.moveaxis(values_in, 1, 0).reshape((heads, blocks, SPAN) + values_in.shape[2:])

    query_c = spanned(queries)
    key_c = spanned(keys)
    value_c = spanned(values)
    beta_c = spanned(strength)
    cumul = jnp.cumsum(spanned(log_decay), axis=-1)
    spread = cumul[..., :, None] - cumul[..., None, :]
    places = jnp.arange(SPAN)
    below = places[:, None] > places[None, :]
    within = places[:, None] >= places[None, :]
    key_dots = jnp.einsum("hnid,hnjd->hnij", key_c, key_c, precision=exact_setting)
    lower_mat = (
        beta_c[..., :, None]
        * jnp.where(below, jnp.exp(jnp.where(below, spread, 0.0)), 0.0)
        * key_dots
    )
    identity_c = jnp.eye(SPAN, dtype=jnp.float32)
    power = lower_mat
    inverse = identity_c - lower_mat
    reach = 1
    while 2 * reach < SPAN:
        power = jnp.einsum("hnij,hnjk->hnik", power, power, precision=exact_setting)
        inverse = jnp.einsum(
            "hnij,hnjk->hnik", inverse, identity_c + power, precision=exact_setting
        )
        reach = reach * 2
    updates = jnp.einsum(
        "hnij,hnjv->hniv", inverse, beta_c[..., None] * value_c, precision=exact_setting
    )
    weights_k = jnp.einsum(
        "hnij,hnjk->hnik",
        inverse,
        (beta_c * jnp.exp(cumul))[..., None] * key_c,
        precision=exact_setting,
    )
    query_dots = jnp.einsum("hnid,hnjd->hnij", query_c, key_c, precision=exact_setting)
    attend = jnp.where(within, jnp.exp(jnp.where(within, spread, 0.0)), 0.0) * query_dots
    query_scaled = jnp.exp(cumul)[..., None] * query_c
    key_end = jnp.exp(cumul[..., -1:] - cumul)[..., None] * key_c
    block_fade = jnp.exp(cumul[..., -1])
    updates_aug = jnp.concatenate(
        [jnp.zeros((heads, blocks, SPAN, KEY_HEAD_SIZE), jnp.float32), updates], -1
    )
    eye_keys = jnp.broadcast_to(
        jnp.eye(KEY_HEAD_SIZE, dtype=jnp.float32), (heads, KEY_HEAD_SIZE, KEY_HEAD_SIZE)
    )
    start_aug = jnp.concatenate([eye_keys, jnp.zeros((heads, KEY_HEAD_SIZE, DV), jnp.float32)], -1)

    def advance(current_state, inputs):
        upd, wgt, qsc, att, kend, fade = inputs
        written = upd - jnp.einsum("hck,hkw->hcw", wgt, current_state, precision=exact_setting)
        readout = jnp.einsum(
            "hck,hkw->hcw", qsc, current_state, precision=exact_setting
        ) + jnp.einsum("hij,hjw->hiw", att, written, precision=exact_setting)
        current_state = fade[:, None, None] * current_state + jnp.einsum(
            "hck,hcw->hkw", kend, written, precision=exact_setting
        )
        return (current_state, readout)

    final_aug, readout_rows = lax.scan(
        advance,
        start_aug,
        (
            to_front(updates_aug),
            to_front(weights_k),
            to_front(query_scaled),
            to_front(attend),
            to_front(key_end),
            to_front(block_fade),
        ),
    )
    readout_rows = jnp.moveaxis(readout_rows, 0, 1).reshape(heads, num_rows, KEY_HEAD_SIZE + DV)
    carry_map = final_aug[..., :KEY_HEAD_SIZE]
    carry_add = final_aug[..., KEY_HEAD_SIZE:]

    def compose(earlier, later):
        return (mat_batch(later[0], earlier[0]), mat_batch(later[0], earlier[1]) + later[1])

    neutral = (eye_keys, jnp.zeros((heads, KEY_HEAD_SIZE, DV), jnp.float32))
    prior_map, prior_add = entering((carry_map, carry_add), "seq", compose, neutral)
    initial_state = mat_batch(prior_map, state_in) + prior_add
    checkpoint = (mat_batch(carry_map, initial_state) + carry_add)[None]
    outputs = readout_rows[..., KEY_HEAD_SIZE:] + jnp.einsum(
        "xlb,xbg->xlg", readout_rows[..., :KEY_HEAD_SIZE], initial_state, precision=exact_setting
    )
    outputs = jnp.moveaxis(outputs, 0, 1)
    gate_z = (
        stored(jnp.dot(hidden_in, w_outgate, preferred_element_type=jnp.float32))
        .astype(jnp.float32)
        .reshape(num_rows, heads, DV)
    )
    scale = lax.rsqrt(jnp.mean(outputs * outputs, axis=-1, keepdims=True) + 1e-06)
    normed = (
        (outputs * scale * norm_gain * jax.nn.silu(gate_z))
        .astype(jnp.bfloat16)
        .reshape(num_rows, heads * DV)
    )
    partial_out = jnp.dot(normed, w_out, preferred_element_type=jnp.float32)
    mixed = lax.psum_scatter(
        partial_out.astype(jnp.bfloat16), "head", scatter_dimension=1, tiled=True
    )
    return (mixed, checkpoint)


def solution(mesh):
    return jax.shard_map(
        local,
        mesh=mesh,
        in_specs=(
            P("seq", None),
            P(None, None, "head"),
            P(None, "head"),
            P(None, "head"),
            P(None, None, "head"),
            P(None, None, "head"),
            P(None, "head"),
            P(None, None, "head"),
            P(None, "head"),
            P("head"),
            P("head"),
            P("head"),
            P("head", None, None),
            P(),
            P("head", None),
        ),
        out_specs=(P("seq", "head"), P("seq", "head", None, None)),
        check_vma=False,
    )
```

profile of v0, /device:TPU:7, one launch (start us, length us, event | category | flops | bytes accessed | tf_op | source)
XLA Modules:
  0.0 361.7 jit_solution(11947911925953387549)
XLA Ops:
  7.2 2.2 copy.80
  12.4 3.5 collective-permute-start
  16.0 1.6 convolution_convert_fusion.4
  20.0 1.3 collective-permute-done
  23.5 1.4 reshape.152
  25.5 1.3 multiply_multiply_fusion
  32.5 1.5 convolution_add_fusion.3
  34.0 1.4 fusion.38
  36.5 2.0 reshape.155
  39.6 1.8 fusion.72
  41.5 1.5 convolution_bitcast_fusion.1
  46.9 1.8 fusion.23
  48.6 28.5 %while.24 = (s32[]{:T(128)}, f32[4,128,256]{2,1,0:T(8,128)S(1)}, f32[4,4,64,256]{3,2,1,0:T(8,128)}, f32[4,4]{1,0:T(4,128)}, f32[4,4,64,128]{3,2,0,1:T(8,128)}, /...) while((s32[]{:T(128)}, f32[4,128,256]{2,1,0:T(8,128)S(1)}, ...), condition=%wide.region_4.5_spmd, body=%wide.region_3.4_spmd.sunk | while | flops 352714752 | bytes 4459673 | solution.py:179
  48.6 1.4 convolution_subtract_fusion.2
  50.1 1.3 fusion.137
  51.4 2.0 fusion.138
  54.1 1.6 convolution_add_fusion.9
  55.8 1.5 convolution_subtract_fusion.2
  57.2 1.3 fusion.137
  58.6 2.0 fusion.138
  61.2 1.6 convolution_add_fusion.9
  62.9 1.5 convolution_subtract_fusion.2
  64.4 1.3 fusion.137
  65.7 2.0 fusion.138
  68.4 1.6 convolution_add_fusion.9
  70.0 1.5 convolution_subtract_fusion.2
  71.5 1.3 fusion.137
  72.8 2.0 fusion.138
  75.5 1.6 convolution_add_fusion.9
  78.7 3.3 convolution_convert_fusion.1
  84.1 2.3 copy.65
  86.4 69.9 %all-gather.5.cloned.1.call-done = bf16[128,128,128]{2,1,0:T(8,128)(2,1)} async-done(((bf16[4,128,128]{2,1,0:T(8,128)(2,1)}), bf16[128,128,128]{2,1,0:T(8,128)(2,1)}) %all-gather.5.cloned.1.call-update) | async-done | bytes 4194320 | tf_op jit(solution)/shard_map/all_gather | solution.py:23
  156.3 82.2 %all-gather.7.cloned.1.call-done = bf16[128,128,128]{2,1,0:T(8,128)(2,1)} async-done(((bf16[4,128,128]{2,1,0:T(8,128)(2,1)}), bf16[128,128,128]{2,1,0:T(8,128)(2,1)}) %all-gather.7.cloned.1.call-update) | async-done | bytes 4194320 | tf_op jit(solution)/shard_map/all_gather | solution.py:23
  238.5 60.9 %while.25 = (s32[]{:T(128)}, f32[4,128,128]{2,1,0:T(8,128)S(1)}, f32[4,128,128]{2,1,0:T(8,128)S(1)}, s32[]{:T(128)}, bf16[32,4,128,128]{3,2,1,0:T(8,128)(2,1)}, ...) while((s32[]{:T(128)}, f32[4,128,128]{2,1,0:T(8,128)S(1)}, ...), condition=%wide.region_6.7_spmd, body=%wide.region_5.6_spmd.sunk | while | flops 201457664 | bytes 2491523 | solution.py:37
  238.5 1.3 convolution_add_fusion.10
  239.8 1.2 fusion.143
  241.1 1.3 convolution_add_fusion.10
  243.6 1.3 convolution_add_fusion.10
  244.9 1.2 fusion.143
  246.2 1.3 convolution_add_fusion.10
  248.7 1.3 convolution_add_fusion.10
  251.2 1.3 convolution_add_fusion.10
  253.8 1.3 convolution_add_fusion.10
  256.3 1.3 convolution_add_fusion.10
  258.9 1.3 convolution_add_fusion.10
  261.4 1.3 convolution_add_fusion.10
  263.9 1.3 convolution_add_fusion.10
  266.5 1.3 convolution_add_fusion.10
  269.0 1.3 convolution_add_fusion.10
  271.6 1.3 convolution_add_fusion.10
  274.1 1.3 convolution_add_fusion.10
  276.6 1.3 convolution_add_fusion.10
  279.2 1.3 convolution_add_fusion.10
  281.7 1.3 convolution_add_fusion.10
  284.2 1.3 convolution_add_fusion.10
  286.8 1.3 convolution_add_fusion.10
  289.3 1.3 convolution_add_fusion.10
  291.9 1.3 convolution_add_fusion.10
  294.4 1.3 convolution_add_fusion.10
  296.9 1.3 convolution_add_fusion.10
  299.5 1.4 convolution_add_fusion.6
  300.9 2.0 multiply_reduce_fusion
  303.2 1.7 convolution_convert_fusion
  306.1 49.1 %reduce-scatter.2.cloned.1.call-done = bf16[256,256]{1,0:T(8,128)(2,1)} async-done(((bf16[256,2048]{1,0:T(8,128)(2,1)}), bf16[256,256]{1,0:T(8,128)(2,1)}) %reduce-scatter.2.cloned.1.call-update) | async-done | bytes 131088 | tf_op jit(solution)/shard_map/reduce_scatter | solution.py:218
  (173 shorter events, 54.5 us)
Async XLA Ops:
  7.2 296.1 %copy-start = (bf16[512,2048]{1,0:T(8,128)(2,1)S(1)}, bf16[512,2048]{1,0:T(8,128)(2,1)}, u32[]{:S(2)}) copy-start(bf16[512,2048]{1,0:T(8,128)(2,1)} %param.33) | copy-start | bytes 6291460
  7.2 149.1 %all-gather.5.cloned.1.call-start = ((), (), s32[]{:S(2)}) async-start(), calls=%async_computation.2 | async-start | bytes 4325376 | tf_op jit(solution)/shard_map/all_gather | solution.py:23
  7.2 2.2 copy-start.4
  9.4 1.6 copy-start.13
  10.2 5.8 %copy-start.7 = (bf16[4,2,256]{2,1,0:T(2,128)(2,1)S(1)}, bf16[4,2,256]{2,1,0:T(2,128)(2,1)}, u32[]{:S(2)}) copy-start(bf16[4,2,256]{2,1,0:T(2,128)(2,1)} %param.24) | copy-start | bytes 12292
  10.2 5.8 %copy-start.5 = (bf16[2048,2,4]{0,2,1:T(4,128)(2,1)S(1)}, bf16[2048,2,4]{0,2,1:T(4,128)(2,1)}, u32[]{:S(2)}) copy-start(bf16[2048,2,4]{0,2,1:T(4,128)(2,1)} %param.23) | copy-start | bytes 98308
  11.0 6.6 %copy-start.14 = (f32[4]{0:T(128)S(1)}, f32[4]{0:T(128)}, u32[]{:S(2)}) copy-start(f32[4]{0:T(128)} %param.28) | copy-start | bytes 52
  11.0 6.6 %copy-start.11 = (f32[4]{0:T(128)S(1)}, f32[4]{0:T(128)}, u32[]{:S(2)}) copy-start(f32[4]{0:T(128)} %param.30) | copy-start | bytes 52
  11.0 6.7 %copy-start.12 = (f32[4]{0:T(128)S(1)}, f32[4]{0:T(128)}, u32[]{:S(2)}) copy-start(f32[4]{0:T(128)} %param.29) | copy-start | bytes 52
  11.0 8.1 %copy-start.6 = (bf16[4,512]{1,0:T(4,128)(2,1)S(1)}, bf16[4,512]{1,0:T(4,128)(2,1)}, u32[]{:S(2)}) copy-start(bf16[4,512]{1,0:T(4,128)(2,1)} %param.25) | copy-start | bytes 12292
  11.0 8.2 %copy-start.9 = (bf16[3,2,256]{2,1,0:T(2,128)(2,1)S(1)}, bf16[3,2,256]{2,1,0:T(2,128)(2,1)}, u32[]{:S(2)}) copy-start(bf16[3,2,256]{2,1,0:T(2,128)(2,1)} %param.26) | copy-start | bytes 9220
  11.8 9.6 %copy-start.8 = (bf16[3,512]{1,0:T(4,128)(2,1)S(1)}, bf16[3,512]{1,0:T(4,128)(2,1)}, u32[]{:S(2)}) copy-start(bf16[3,512]{1,0:T(4,128)(2,1)} %param.27) | copy-start | bytes 9220
  12.4 9.0 %collective-permute-start = (bf16[3,1024]{1,0:T(4,128)(2,1)}, bf16[3,1024]{1,0:T(4,128)(2,1)S(1)}, u32[]{:S(2)}, u32[]{:S(2)}) collective-permute-start(bf16[3,1024]{1,0:T(4,128)(2,1)} %pad_maximum_fusion), channel_id=1, source_target_pairs={{0,8},{8,16},{16,24},{24,32},{32,40},{40,48},{48,56},{56,64},{64,7... | collective-permute-start | bytes 18440 | tf_op jit(solution)/shard_map/ppermute | solution.py:17
  31.8 3.6 copy-start.1
  41.5 3.3 copy-start.3
  77.9 160.6 %all-gather.7.cloned.1.call-start = ((), (), s32[]{:S(2)}) async-start(), calls=%async_computation.3 | async-start | bytes 4325376 | tf_op jit(solution)/shard_map/all_gather | solution.py:23
  78.7 276.5 %reduce-scatter.2.cloned.1.call-start = ((), (), s32[]{:S(2)}) async-start(), calls=%async_computation.1 | async-start | bytes 1179648 | tf_op jit(solution)/shard_map/reduce_scatter | solution.py:218
  299.4 3.4 copy-start.2
  299.5 3.4 copy-start.10
Sparse Core Ops, SparseCore 0:
  78.0 78.2 all-gather.4
  159.4 78.9 all-gather.6
  305.1 49.9 reduce-scatter.1
where the time goes:
time: 366 us; the launch traced here: 362 us
  waiting for transfers between devices  203 us (55%)
  matrix products  111 us (30%)
  local copies, waits for them, and re-layouts  18.8 us (5%)
  between operations  14.3 us (4%)
  other arithmetic  9.23 us (3%)
    all_gather x2, waiting for transfers between devices, entering(): lax.all_gather(a.astype(kind), axis)  152 us
    dot_general x50, matrix products, mat_batch(): return jnp.einsum('hij,hjk->hik', left, right, precision=exact_setting)  61.2 us
    reduce_scatter x1, waiting for transfers between devices, local(): lax.psum_scatter(partial_out.astype(jnp.bfloat16), 'head', scatter_dimens...  49.1 us
    dot_general x4, matrix products, advance(): jnp.einsum('hij,hjw->hiw', att, written, precision=exact_setting)  7.93 us
  transfers between devices with their start and end apart: 4, of which 4 were waited for; matrix products, arithmetic and copies ran while one was open for 4% of the time, Pallas kernels for 0%

commit v1 on v0

--- a/solution.py
+++ b/solution.py
@@ -15,26 +15,6 @@
     count = lax.axis_size(axis)
     leading, last = (max(0, -steps), min(count, count - steps))
     return lax.ppermute(value, axis, [(source, source + steps) for source in range(leading, last)])
-
-
-def entering(value, axis, join, neutral):
-    place = lax.axis_index(axis)
-    gathered = jax.tree.map(
-        lambda a, kind: lax.all_gather(a.astype(kind), axis), value, (jnp.bfloat16, jnp.bfloat16)
-    )
-    state = jax.tree.map(lambda a, e: jnp.zeros_like(a) + jnp.asarray(e, a.dtype), value, neutral)
-
-    def one(turn, state):
-        return join(
-            state,
-            jax.tree.map(
-                lambda a, own: lax.dynamic_index_in_dim(a, turn, 0, False).astype(own.dtype),
-                gathered,
-                value,
-            ),
-        )
-
-    return lax.fori_loop(0, place, one, state)
 
 
 def stored(values):
@@ -192,13 +172,23 @@
     carry_map = final_aug[..., :KEY_HEAD_SIZE]
     carry_add = final_aug[..., KEY_HEAD_SIZE:]
 
-    def compose(earlier, later):
-        return (mat_batch(later[0], earlier[0]), mat_batch(later[0], earlier[1]) + later[1])
-
-    neutral = (eye_keys, jnp.zeros((heads, KEY_HEAD_SIZE, DV), jnp.float32))
-    prior_map, prior_add = entering((carry_map, carry_add), "seq", compose, neutral)
-    initial_state = mat_batch(prior_map, state_in) + prior_add
-    checkpoint = (mat_batch(carry_map, initial_state) + carry_add)[None]
+    span_add = jnp.where(leading, mat_batch(carry_map, state_in) + carry_add, carry_add)
+    span_map = jnp.where(leading, 0.0, carry_map)
+    count = lax.axis_size("seq")
+    reach = 1
+    while 2 * reach < count:
+        both = jnp.concatenate([span_map, span_add], -1).astype(jnp.bfloat16)
+        came = shifted(both, "seq", reach).astype(jnp.float32)
+        joined = mat_batch(span_map, came)
+        has_left = lax.axis_index("seq") >= reach
+        span_add = joined[..., KEY_HEAD_SIZE:] + span_add
+        span_map = jnp.where(has_left, joined[..., :KEY_HEAD_SIZE], span_map)
+        reach = reach * 2
+    came = shifted(span_add.astype(jnp.bfloat16), "seq", reach).astype(jnp.float32)
+    span_add = mat_batch(span_map, came) + span_add
+    checkpoint = span_add[None]
+    came = shifted(span_add.astype(jnp.bfloat16), "seq", 1).astype(jnp.float32)
+    initial_state = jnp.where(leading, state_in, came)
     outputs = readout_rows[..., KEY_HEAD_SIZE:] + jnp.einsum(
         "xlb,xbg->xlg", readout_rows[..., :KEY_HEAD_SIZE], initial_state, precision=exact_setting
     )
@@ -215,9 +205,10 @@
         .reshape(num_rows, heads * DV)
     )
     partial_out = jnp.dot(normed, w_out, preferred_element_type=jnp.float32)
-    mixed = lax.psum_scatter(
-        partial_out.astype(jnp.bfloat16), "head", scatter_dimension=1, tiled=True
-    )
+    groups = lax.axis_size("head")
+    terms = partial_out.astype(jnp.bfloat16).reshape(num_rows, groups, -1)
+    terms = lax.all_to_all(terms, "head", 1, 0, tiled=False)
+    mixed = jnp.sum(terms.astype(jnp.float32), axis=0).astype(jnp.bfloat16)
     return (mixed, checkpoint)
 
 

time: 366 us -> 190 us (0.52)
  waiting for transfers between devices: 203 us -> 56.7 us
  matrix products: 111 us -> 53.9 us
  blocking collectives: 0 us -> 23 us
  between operations: 14.3 us -> 1.31 us
  starting transfers between devices: 3.65 us -> 15.5 us
  other arithmetic: 9.23 us -> 17.1 us
    all_gather x2 -> x0, waiting for transfers between devices: 152 us -> none  [entering(): lax.all_gather(a.astype(kind), axis)]
    ppermute x1 -> x7, waiting for transfers between devices: 1.34 us -> 56.7 us  [shifted(): lax.ppermute(value, axis, [(source, source + steps) for source in range(l...]
    dot_general x50 -> x6, matrix products: 61.2 us -> 6.68 us  [mat_batch(): return jnp.einsum('hij,hjk->hik', left, right, precision=exact_setting)]
    reduce_scatter x1 -> x0, waiting for transfers between devices: 49.1 us -> none  [local(): lax.psum_scatter(partial_out.astype(jnp.bfloat16), 'head', scatter_dimens...]
    all_to_all x0 -> x1, blocking collectives: none -> 23 us  [local(): terms = lax.all_to_all(terms, 'head', 1, 0, tiled=False)]
    ppermute x1 -> x7, starting transfers between devices: 3.53 us -> 15.5 us  [shifted(): lax.ppermute(value, axis, [(source, source + steps) for source in range(l...]
    unnamed x36 -> x39, local copies, waits for them, and re-layouts: 3.11 us -> 7.59 us
  transfers between devices with their start and end apart: 4 -> 7, of which waited for: 4 -> 6; matrix products, arithmetic and copies ran while one was open for 4% -> 9% of each run, Pallas kernels for 0% -> 0%
where the time goes in v1:
time: 190 us; the launch traced here: 188 us
  waiting for transfers between devices  56.7 us (30%)
  matrix products  53.9 us (28%)
  blocking collectives  23 us (12%)
  local copies, waits for them, and re-layouts  20.5 us (11%)
  other arithmetic  17.1 us (9%)
  starting transfers between devices  15.5 us (8%)
    ppermute x7, waiting for transfers between devices, shifted(): lax.ppermute(value, axis, [(source, source + steps) for source in range(l...  56.7 us
    all_to_all x1, blocking collectives, local(): terms = lax.all_to_all(terms, 'head', 1, 0, tiled=False)  23 us
    ppermute x7, starting transfers between devices, shifted(): lax.ppermute(value, axis, [(source, source + steps) for source in range(l...  15.5 us
    dot_general x4, matrix products, advance(): jnp.einsum('hij,hjw->hiw', att, written, precision=exact_setting)  7.88 us
    unnamed x39, local copies, waits for them, and re-layouts  7.59 us
    dot_general x6, matrix products, mat_batch(): return jnp.einsum('hij,hjk->hik', left, right, precision=exact_setting)  6.68 us
    dot_general x4, matrix products, advance(): jnp.einsum('hck,hcw->hkw', kend, written, precision=exact_setting)  6.57 us
    dot_general x4, matrix products, advance(): jnp.einsum('hck,hkw->hcw', wgt, current_state, precision=exact_setting)  5.83 us
  transfers between devices with their start and end apart: 7, of which 6 were waited for; matrix products, arithmetic and copies ran while one was open for 9% of the time, Pallas kernels for 0%

profile of v1, /device:TPU:7, one launch (start us, length us, event | category | flops | bytes accessed | tf_op | source)
XLA Modules:
  0.0 188.0 jit_solution(15638587508940733508)
XLA Ops:
  0.7 2.2 %copy.89 = bf16[256,8,2,256]{3,1,2,0:T(8,128)(2,1)S(1)} copy(bf16[256,8,2,256]{3,2,1,0:T(2,128)(2,1)} %bitcast.199) | data formatting | bytes 4194304
  3.6 0.8 copy-done.15
  5.9 3.5 %collective-permute-start = (bf16[3,1024]{1,0:T(4,128)(2,1)}, bf16[3,1024]{1,0:T(4,128)(2,1)}, u32[]{:S(2)}, u32[]{:S(2)}) collective-permute-start(bf16[3,1024]{1,0:T(4,128)(2,1)} %pad_maximum_fusion.4), channel_id=1, source_target_pairs={{0,8},{8,16},{16,24},{24,32},{32,40},{40,48},{48,56},{56,64},{64,7... | collective-permute-start | bytes 18440 | tf_op jit(solution)/shard_map/ppermute | solution.py:17
  10.1 0.8 reshape.145
  10.8 1.0 convolution_convert_fusion.4
  14.1 0.9 reduce_window_sum.11
  15.9 1.4 slice_convert_fusion.3
  22.2 1.9 maximum_convert_fusion
  24.1 1.1 divide_multiply_fusion.1
  25.2 1.4 reshape.151
  27.3 0.9 multiply_multiply_fusion
  28.3 1.0 convolution_multiply_fusion
  33.9 1.4 convolution_add_fusion.2
  35.3 1.5 fusion.31
  36.8 1.1 divide_multiply_fusion
  37.9 2.0 %reshape.154 = f32[256,4,128]{2,1,0:T(4,128)} reshape(f32[256,512]{1,0:T(8,128)} %divide_multiply_fusion) | data formatting | bytes 1048576 | tf_op jit(solution)/shard_map/reshape | solution.py:81
  40.0 1.1 copy.58
  41.0 1.8 fusion.82
  42.9 1.5 convolution_bitcast_fusion.1
  45.1 1.1 pad_bitcast_fusion
  46.2 1.0 multiply_bitcast_fusion.1
  47.2 1.0 multiply_bitcast_fusion
  48.2 1.7 fusion.16
  50.0 28.5 %while.12 = (s32[]{:T(128)}, f32[4,128,256]{2,1,0:T(8,128)S(1)}, f32[4,4,64,256]{3,2,1,0:T(8,128)}, f32[4,4]{1,0:T(4,128)}, f32[4,4,64,128]{3,2,0,1:T(8,128)}, /...) while((s32[]{:T(128)}, f32[4,128,256]{2,1,0:T(8,128)S(1)}, ...), condition=%wide.region_4.5_spmd, body=%wide.region_3.4_spmd.sunk | while | flops 352714752 | bytes 4459673 | solution.py:159
  50.0 1.5 convolution_subtract_fusion.2
  51.4 1.3 fusion.148
  52.8 2.0 %fusion.149 = f32[4,4,64,256]{3,2,1,0:T(8,128)} fusion(f32[4,4,64,256]{3,2,1,0:T(8,128)} %get-tuple-element.203, s32[]{:T(128)} %get-tuple-element.201, f32[4,64,256]{2,1,0:T(8,128)S(1)} %fusion.148, f32[4,64,256]{2,1,0:T(8,128)S(1)} %convolution_subtract_fusion.2, f32[4,4,64,64]{3,2,1,0:T(8,128)} %get-tuple-element.219), kind=kOutput, calls=%fused_computation.3.clone.1 | convolution fusion | flops 50397184 | bytes 918528 | tf_op jit(solution)/shard_map/while/body/eval_jaxpr/hij,hjw->hiw/dot_general | solution.py:153
  55.4 1.6 convolution_add_fusion.7
  57.1 1.5 convolution_subtract_fusion.2
  58.6 1.3 fusion.148
  59.9 2.0 %fusion.149 = f32[4,4,64,256]{3,2,1,0:T(8,128)} fusion(f32[4,4,64,256]{3,2,1,0:T(8,128)} %get-tuple-element.203, s32[]{:T(128)} %get-tuple-element.201, f32[4,64,256]{2,1,0:T(8,128)S(1)} %fusion.148, f32[4,64,256]{2,1,0:T(8,128)S(1)} %convolution_subtract_fusion.2, f32[4,4,64,64]{3,2,1,0:T(8,128)} %get-tuple-element.219), kind=kOutput, calls=%fused_computation.3.clone.1 | convolution fusion | flops 50397184 | bytes 918528 | tf_op jit(solution)/shard_map/while/body/eval_jaxpr/hij,hjw->hiw/dot_general | solution.py:153
  62.5 1.6 convolution_add_fusion.7
  64.2 1.5 convolution_subtract_fusion.2
  65.7 1.3 fusion.148
  67.0 2.0 %fusion.149 = f32[4,4,64,256]{3,2,1,0:T(8,128)} fusion(f32[4,4,64,256]{3,2,1,0:T(8,128)} %get-tuple-element.203, s32[]{:T(128)} %get-tuple-element.201, f32[4,64,256]{2,1,0:T(8,128)S(1)} %fusion.148, f32[4,64,256]{2,1,0:T(8,128)S(1)} %convolution_subtract_fusion.2, f32[4,4,64,64]{3,2,1,0:T(8,128)} %get-tuple-element.219), kind=kOutput, calls=%fused_computation.3.clone.1 | convolution fusion | flops 50397184 | bytes 918528 | tf_op jit(solution)/shard_map/while/body/eval_jaxpr/hij,hjw->hiw/dot_general | solution.py:153
  69.7 1.6 convolution_add_fusion.7
  71.3 1.5 convolution_subtract_fusion.2
  72.8 1.3 fusion.148
  74.1 2.0 %fusion.149 = f32[4,4,64,256]{3,2,1,0:T(8,128)} fusion(f32[4,4,64,256]{3,2,1,0:T(8,128)} %get-tuple-element.203, s32[]{:T(128)} %get-tuple-element.201, f32[4,64,256]{2,1,0:T(8,128)S(1)} %fusion.148, f32[4,64,256]{2,1,0:T(8,128)S(1)} %convolution_subtract_fusion.2, f32[4,4,64,64]{3,2,1,0:T(8,128)} %get-tuple-element.219), kind=kOutput, calls=%fused_computation.3.clone.1 | convolution fusion | flops 50397184 | bytes 918528 | tf_op jit(solution)/shard_map/while/body/eval_jaxpr/hij,hjw->hiw/dot_general | solution.py:153
  76.8 1.6 convolution_add_fusion.7
  78.9 3.6 %collective-permute-start.1 = (bf16[4,128,256]{2,1,0:T(8,128)(2,1)S(1)}, bf16[4,128,256]{2,1,0:T(8,128)(2,1)}, u32[]{:S(2)}, u32[]{:S(2)}) collective-permute-start(bf16[4,128,256]{2,1,0:T(8,128)(2,1)S(1)} %pad_maximum_fusion), channel_id=1, source_target_pairs={{0,8},{8,16},{16,24},{24,32},{32,40},{40,48},{48,56},{56,64},{64,7... | collective-permute-start | bytes 786440 | tf_op jit(solution)/shard_map/ppermute | solution.py:17
  82.5 8.7 %collective-permute-done.1 = bf16[4,128,256]{2,1,0:T(8,128)(2,1)} collective-permute-done((bf16[4,128,256]{2,1,0:T(8,128)(2,1)S(1)}, bf16[4,128,256]{2,1,0:T(8,128)(2,1)}, u32[]{:S(2)}, u32[]{:S(2)}) %collective-permute-start.1) | collective-permute-done | bytes 262176 | tf_op jit(solution)/shard_map/ppermute | solution.py:17
  91.2 1.3 fusion.49
  92.5 0.8 fusion.74
  93.3 2.0 %collective-permute-start.2 = (bf16[4,128,256]{2,1,0:T(8,128)(2,1)S(1)}, bf16[4,128,256]{2,1,0:T(8,128)(2,1)S(1)}, u32[]{:S(2)}, u32[]{:S(2)}) collective-permute-start(bf16[4,128,256]{2,1,0:T(8,128)(2,1)S(1)} %pad_maximum_fusion.1), channel_id=1, source_target_pairs={{0,16},{8,24},{16,32},{24,40},{32,48},{40,56},{48,64},{56,72},{64,... | collective-permute-start | bytes 786440 | tf_op jit(solution)/shard_map/ppermute | solution.py:17
  95.3 14.3 %collective-permute-done.2 = bf16[4,128,256]{2,1,0:T(8,128)(2,1)S(1)} collective-permute-done((bf16[4,128,256]{2,1,0:T(8,128)(2,1)S(1)}, bf16[4,128,256]{2,1,0:T(8,128)(2,1)S(1)}, u32[]{:S(2)}, u32[]{:S(2)}) %collective-permute-start.2) | collective-permute-done | bytes 262176 | tf_op jit(solution)/shard_map/ppermute | solution.py:17
  109.7 1.3 fusion.83
  111.0 0.8 fusion.72
  111.8 1.9 %collective-permute-start.3 = (bf16[4,128,256]{2,1,0:T(8,128)(2,1)S(1)}, bf16[4,128,256]{2,1,0:T(8,128)(2,1)S(1)}, u32[]{:S(2)}, u32[]{:S(2)}) collective-permute-start(bf16[4,128,256]{2,1,0:T(8,128)(2,1)S(1)} %pad_maximum_fusion.2), channel_id=1, source_target_pairs={{0,32},{8,40},{16,48},{24,56},{32,64},{40,72},{48,80},{56,88},{64,... | collective-permute-start | bytes 786440 | tf_op jit(solution)/shard_map/ppermute | solution.py:17
  113.8 18.1 %collective-permute-done.3 = bf16[4,128,256]{2,1,0:T(8,128)(2,1)S(1)} collective-permute-done((bf16[4,128,256]{2,1,0:T(8,128)(2,1)S(1)}, bf16[4,128,256]{2,1,0:T(8,128)(2,1)S(1)}, u32[]{:S(2)}, u32[]{:S(2)}) %collective-permute-start.3) | collective-permute-done | bytes 262176 | tf_op jit(solution)/shard_map/ppermute | solution.py:17
  131.9 1.3 fusion.84
  133.3 1.3 collective-permute-start.4
  134.6 8.0 %collective-permute-done.4 = bf16[4,128,256]{2,1,0:T(8,128)(2,1)S(1)} collective-permute-done((bf16[4,128,256]{2,1,0:T(8,128)(2,1)S(1)}, bf16[4,128,256]{2,1,0:T(8,128)(2,1)S(1)}, u32[]{:S(2)}, u32[]{:S(2)}) %collective-permute-start.4) | collective-permute-done | bytes 262176 | tf_op jit(solution)/shard_map/ppermute | solution.py:17
  142.9 0.8 copy-done.2
  143.8 1.3 collective-permute-start.5
  145.1 5.9 %collective-permute-done.5 = bf16[4,128,128]{2,1,0:T(8,128)(2,1)S(1)} collective-permute-done((bf16[4,128,128]{2,1,0:T(8,128)(2,1)S(1)}, bf16[4,128,128]{2,1,0:T(8,128)(2,1)S(1)}, u32[]{:S(2)}, u32[]{:S(2)}) %collective-permute-start.5) | collective-permute-done | bytes 131104 | tf_op jit(solution)/shard_map/ppermute | solution.py:17
  151.0 2.0 %fusion.77 = (bf16[4,128,128]{2,1,0:T(8,128)(2,1)S(1)}, f32[4,128,128]{2,1,0:T(8,128)}) fusion(f32[4,128,128]{2,1,0:T(8,128)S(1)} %get-tuple-element.109, f32[4,128,256]{2,1,0:T(8,128)S(1)} %fusion.84, f32[4,128,256]{2,1,0:T(8,128)} %copy-done.2, bf16[4,128,128]{2,1,0:T(8,128)(2,1)S(1)} %collective-permute-done.5, ...), kind=kOutput, calls=%fused_computation.154 | convolution fusion | flops 100990976 | bytes 1835009 | tf_op jit(solution)/shard_map/hij,hjk->hik/dot_general | solution.py:38
  153.0 1.9 %collective-permute-start.6 = (bf16[4,128,128]{2,1,0:T(8,128)(2,1)S(1)}, bf16[4,128,128]{2,1,0:T(8,128)(2,1)}, u32[]{:S(2)}, u32[]{:S(2)}) collective-permute-start(bf16[4,128,128]{2,1,0:T(8,128)(2,1)S(1)} %get-tuple-element.130), channel_id=1, source_target_pairs={{0,8},{8,16},{16,24},{24,32},{32,40},{40,48},{48,56},{56,64},{64,7... | collective-permute-start | bytes 393224 | tf_op jit(solution)/shard_map/ppermute | solution.py:17
  154.9 2.6 %convolution_convert_fusion.1 = bf16[256,512]{1,0:T(8,128)(2,1)S(1)} fusion(bf16[256,2048]{1,0:T(8,128)(2,1)} %param.17, bf16[2048,512]{1,0:T(8,128)(2,1)} %param.20), kind=kOutput, calls=%fused_computation.28 | convolution fusion | flops 537001984 | bytes 3407872 | tf_op jit(solution)/shard_map/dot_general | solution.py:197
  157.9 1.3 copy.69
  159.3 1.7 collective-permute-done.6
  160.9 1.7 multiply_reduce_fusion
  164.3 23.0 %all_to_all.4 = bf16[1,256,8,256]{3,1,0,2:T(8,128)(2,1)S(1)} all-to-all(bf16[1,256,8,256]{3,1,0,2:T(8,128)(2,1)S(1)} %copy.78), channel_id=1, replica_groups=mesh['seq'=32,'head'=8] {'head'}, dimensions={2} | all-to-all | bytes 2097152 | tf_op jit(solution)/shard_map/all_to_all | solution.py:210
  187.2 0.8 reduce_sum.42
  (96 shorter events, 22.4 us)
Async XLA Ops:
  0.6 162.4 %copy-start = (bf16[512,2048]{1,0:T(8,128)(2,1)S(1)}, bf16[512,2048]{1,0:T(8,128)(2,1)}, u32[]{:S(2)}) copy-start(bf16[512,2048]{1,0:T(8,128)(2,1)} %param.31) | copy-start | bytes 6291460
  0.6 2.2 %copy-start.3 = (bf16[256,2048]{1,0:T(8,128)(2,1)S(1)}, bf16[256,2048]{1,0:T(8,128)(2,1)}, u32[]{:S(2)}) copy-start(bf16[256,2048]{1,0:T(8,128)(2,1)} %param.17) | copy-start | bytes 3145732
  2.9 1.6 copy-start.15
  3.6 5.9 %copy-start.13 = (bf16[4,2,256]{2,1,0:T(2,128)(2,1)S(1)}, bf16[4,2,256]{2,1,0:T(2,128)(2,1)}, u32[]{:S(2)}) copy-start(bf16[4,2,256]{2,1,0:T(2,128)(2,1)} %param.22) | copy-start | bytes 12292
  5.2 4.2 %copy-start.6 = (bf16[256,512]{1,0:T(8,128)(2,1)}, bf16[256,512]{1,0:T(8,128)(2,1)S(1)}, u32[]{:S(2)}) copy-start(bf16[256,512]{1,0:T(8,128)(2,1)S(1)} %convolution_convert_fusion.2) | copy-start | bytes 786436
  5.9 15.6 %collective-permute-start = (bf16[3,1024]{1,0:T(4,128)(2,1)}, bf16[3,1024]{1,0:T(4,128)(2,1)}, u32[]{:S(2)}, u32[]{:S(2)}) collective-permute-start(bf16[3,1024]{1,0:T(4,128)(2,1)} %pad_maximum_fusion.4), channel_id=1, source_target_pairs={{0,8},{8,16},{16,24},{24,32},{32,40},{40,48},{48,56},{56,64},{64,7... | collective-permute-start | bytes 18440 | tf_op jit(solution)/shard_map/ppermute | solution.py:17
  33.2 3.6 %copy-start.1 = (f32[259,512]{1,0:T(8,128)S(1)}, f32[259,512]{1,0:T(8,128)}, u32[]{:S(2)}) copy-start(f32[259,512]{1,0:T(8,128)} %get-tuple-element.135) | copy-start | bytes 1591300
  33.2 3.6 %copy-start.9 = (f32[1,512]{1,0:T(1,128)S(1)}, f32[1,512]{1,0:T(1,128)}, u32[]{:S(2)}) copy-start(f32[1,512]{1,0:T(1,128)} %get-tuple-element.120) | copy-start | bytes 6148
  33.2 3.6 %copy-start.10 = (f32[1,512]{1,0:T(1,128)S(1)}, f32[1,512]{1,0:T(1,128)}, u32[]{:S(2)}) copy-start(f32[1,512]{1,0:T(1,128)} %get-tuple-element.121) | copy-start | bytes 6148
  33.2 3.6 %copy-start.11 = (f32[1,512]{1,0:T(1,128)S(1)}, f32[1,512]{1,0:T(1,128)}, u32[]{:S(2)}) copy-start(f32[1,512]{1,0:T(1,128)} %get-tuple-element.122) | copy-start | bytes 6148
  33.2 3.6 %copy-start.12 = (f32[1,512]{1,0:T(1,128)S(1)}, f32[1,512]{1,0:T(1,128)}, u32[]{:S(2)}) copy-start(f32[1,512]{1,0:T(1,128)} %get-tuple-element.123) | copy-start | bytes 6148
  37.9 4.9 %copy-start.8 = (f32[4,4,64]{2,1,0:T(4,128)S(1)}, f32[4,4,64]{2,1,0:T(4,128)}, u32[]{:S(2)}) copy-start(f32[4,4,64]{2,1,0:T(4,128)} %get-tuple-element.114) | copy-start | bytes 12292
  42.9 3.3 %copy-start.7 = (f32[4,4,64]{2,1,0:T(4,128)S(1)}, f32[4,4,64]{2,1,0:T(4,128)}, u32[]{:S(2)}) copy-start(f32[4,4,64]{2,1,0:T(4,128)} %get-tuple-element.115) | copy-start | bytes 12292
  50.0 28.5 %copy-start.4 = (f32[4,128,128]{2,1,0:T(8,128)S(1)}, f32[4,128,128]{2,1,0:T(8,128)}, u32[]{:S(2)}) copy-start(f32[4,128,128]{2,1,0:T(8,128)} %param.29) | copy-start | bytes 786436
  78.9 12.3 %collective-permute-start.1 = (bf16[4,128,256]{2,1,0:T(8,128)(2,1)S(1)}, bf16[4,128,256]{2,1,0:T(8,128)(2,1)}, u32[]{:S(2)}, u32[]{:S(2)}) collective-permute-start(bf16[4,128,256]{2,1,0:T(8,128)(2,1)S(1)} %pad_maximum_fusion), channel_id=1, source_target_pairs={{0,8},{8,16},{16,24},{24,32},{32,40},{40,48},{48,56},{56,64},{64,7... | collective-permute-start | bytes 786440 | tf_op jit(solution)/shard_map/ppermute | solution.py:17
  93.3 16.4 %collective-permute-start.2 = (bf16[4,128,256]{2,1,0:T(8,128)(2,1)S(1)}, bf16[4,128,256]{2,1,0:T(8,128)(2,1)S(1)}, u32[]{:S(2)}, u32[]{:S(2)}) collective-permute-start(bf16[4,128,256]{2,1,0:T(8,128)(2,1)S(1)} %pad_maximum_fusion.1), channel_id=1, source_target_pairs={{0,16},{8,24},{16,32},{24,40},{32,48},{40,56},{48,64},{56,72},{64,... | collective-permute-start | bytes 786440 | tf_op jit(solution)/shard_map/ppermute | solution.py:17
  111.8 20.0 %collective-permute-start.3 = (bf16[4,128,256]{2,1,0:T(8,128)(2,1)S(1)}, bf16[4,128,256]{2,1,0:T(8,128)(2,1)S(1)}, u32[]{:S(2)}, u32[]{:S(2)}) collective-permute-start(bf16[4,128,256]{2,1,0:T(8,128)(2,1)S(1)} %pad_maximum_fusion.2), channel_id=1, source_target_pairs={{0,32},{8,40},{16,48},{24,56},{32,64},{40,72},{48,80},{56,88},{64,... | collective-permute-start | bytes 786440 | tf_op jit(solution)/shard_map/ppermute | solution.py:17
  133.3 9.3 %collective-permute-start.4 = (bf16[4,128,256]{2,1,0:T(8,128)(2,1)S(1)}, bf16[4,128,256]{2,1,0:T(8,128)(2,1)S(1)}, u32[]{:S(2)}, u32[]{:S(2)}) collective-permute-start(bf16[4,128,256]{2,1,0:T(8,128)(2,1)S(1)} %pad_maximum_fusion.3), channel_id=1, source_target_pairs={{0,64},{8,72},{16,80},{24,88},{32,96},{40,104},{48,112},{56,120},{... | collective-permute-start | bytes 786440 | tf_op jit(solution)/shard_map/ppermute | solution.py:17
  142.9 0.8 copy-start.2
  143.8 7.2 %collective-permute-start.5 = (bf16[4,128,128]{2,1,0:T(8,128)(2,1)S(1)}, bf16[4,128,128]{2,1,0:T(8,128)(2,1)S(1)}, u32[]{:S(2)}, u32[]{:S(2)}) collective-permute-start(bf16[4,128,128]{2,1,0:T(8,128)(2,1)S(1)} %fusion.70), channel_id=1, source_target_pairs={{0,128},{8,136},{16,144},{24,152},{32,160},{40,168},{48,176},{56,1... | collective-permute-start | bytes 393224 | tf_op jit(solution)/shard_map/ppermute | solution.py:17
  153.0 7.9 %collective-permute-start.6 = (bf16[4,128,128]{2,1,0:T(8,128)(2,1)S(1)}, bf16[4,128,128]{2,1,0:T(8,128)(2,1)}, u32[]{:S(2)}, u32[]{:S(2)}) collective-permute-start(bf16[4,128,128]{2,1,0:T(8,128)(2,1)S(1)} %get-tuple-element.130), channel_id=1, source_target_pairs={{0,8},{8,16},{16,24},{24,32},{32,40},{40,48},{48,56},{56,64},{64,7... | collective-permute-start | bytes 393224 | tf_op jit(solution)/shard_map/ppermute | solution.py:17
  157.6 3.4 %copy-start.5 = (f32[4,128,128]{2,1,0:T(8,128)S(1)}, f32[4,128,128]{2,1,0:T(8,128)}, u32[]{:S(2)}) copy-start(f32[4,128,128]{2,1,0:T(8,128)} %param.29) | copy-start | bytes 786436
  157.7 4.9 %copy-start.14 = (f32[128]{0:T(128)S(1)}, f32[128]{0:T(128)}, u32[]{:S(2)}) copy-start(f32[128]{0:T(128)} %param.30) | copy-start | bytes 1540

commit v2 on v1

v2 whole, which is shorter than its diff:
```python
import functools

import jax
import jax.numpy as jnp
from jax import lax
from jax.experimental import pallas as pl
from jax.experimental.pallas import tpu as pltpu
from jax.sharding import PartitionSpec as P

KEY_HEAD_SIZE = 128
DV = 128
SPAN = 128
EDGE = 8


exact_setting = lax.Precision.HIGHEST


def half(values):
    return values.astype(jnp.bfloat16)


def mm(left, right, dims=((1,), (0,))):
    return lax.dot_general(half(left), half(right), (dims, ((), ())), preferred_element_type=jnp.float32)


def silu(values):
    return values / (1.0 + jnp.exp(-values))


def shifted(value, axis, steps):
    count = lax.axis_size(axis)
    leading, last = (max(0, -steps), min(count, count - steps))
    return lax.ppermute(value, axis, [(source, source + steps) for source in range(leading, last)])


def stored(values):
    return lax.optimization_barrier(values.astype(jnp.bfloat16))


def mat_batch(left, right):
    return jnp.einsum("hij,hjk->hik", left, right, precision=exact_setting)


def filtered(rim_ref, present_ref, weight_ref, room):
    count, width = present_ref.shape
    taps = weight_ref.shape[0]
    room[:EDGE, :width] = rim_ref[...].astype(jnp.float32)
    room[EDGE:, :width] = present_ref[...].astype(jnp.float32)
    first = EDGE - (taps - 1)
    total = jnp.zeros((count, width), jnp.float32)
    for tap in range(taps):
        weight = weight_ref[tap : tap + 1, :].astype(jnp.float32)
        total = total + weight * room[first + tap : first + tap + count, :width]
    return silu(total)


def unit_rows(values):
    return values * lax.rsqrt(jnp.sum(values * values, axis=-1, keepdims=True) + 1e-06)


def unit_inverses(lowers, row, col):
    size = row.shape[0]
    eye = jnp.where(row == col, 1.0, 0.0)
    step = 1
    results = None
    while step < size:
        pair = jnp.logical_and(row // (2 * step) == col // (2 * step), row // step > col // step)
        cross = [jnp.where(pair, lower, 0.0) for lower in lowers]
        if results is None:
            results = [eye - c for c in cross]
        else:
            inner = [mm(c, x) for c, x in zip(cross, results)]
            results = [x - mm(x, y) for x, y in zip(results, inner)]
        step = 2 * step
    return results


def block_kernel(
    q_rim, q_new, q_taps, k_rim, k_new, k_taps, v_rim, v_new, v_taps,
    beta_ref, cumul_ref, turned_ref, maps_ref, base_ref, slope_ref, room,
):
    queries = unit_rows(filtered(q_rim, q_new, q_taps, room)) * KEY_HEAD_SIZE ** (-0.5)
    keys = unit_rows(filtered(k_rim, k_new, k_taps, room))
    values = filtered(v_rim, v_new, v_taps, room)
    count = queries.shape[0]
    ratio = values.shape[1] // DV
    blocks = count // SPAN
    row = lax.broadcasted_iota(jnp.int32, (SPAN, SPAN), 0)
    col = lax.broadcasted_iota(jnp.int32, (SPAN, SPAN), 1)
    jobs = []
    for n in range(blocks):
        rows = slice(n * SPAN, (n + 1) * SPAN)
        query, key = queries[rows], keys[rows]
        key_dots = mm(key, key, ((1,), (1,)))
        query_dots = mm(query, key, ((1,), (1,)))
        for h in range(ratio):
            beta = beta_ref[0, rows, h : h + 1]
            cumul = cumul_ref[0, rows, h : h + 1]
            turned = turned_ref[0, h : h + 1, rows]
            last = turned[:, SPAN - 1 :]
            fading = jnp.exp(jnp.where(row >= col, cumul - turned, 0.0))
            grown = jnp.exp(cumul)
            jobs.append(
                dict(
                    n=n,
                    h=h,
                    rows=rows,
                    lower=jnp.where(row > col, beta * fading * key_dots, 0.0),
                    attend=jnp.where(row >= col, fading * query_dots, 0.0),
                    sides=jnp.concatenate(
                        [beta * grown * key, beta * values[rows, h * DV : (h + 1) * DV]], 1
                    ),
                    query=grown * query,
                    key_end=jnp.exp(last - cumul) * key,
                    fade=jnp.exp(last),
                )
            )
    inverses = unit_inverses([job["lower"] for job in jobs], row, col)
    solved = [mm(inverse, job["sides"]) for inverse, job in zip(inverses, jobs)]
    eye = jnp.where(row == col, 1.0, 0.0)
    none = jnp.zeros((SPAN, DV), jnp.float32)
    state = [None] * ratio
    for job, both in zip(jobs, solved):
        h, rows = job["h"], job["rows"]
        weights, updates = both[:, :KEY_HEAD_SIZE], both[:, KEY_HEAD_SIZE:]
        if job["n"] == 0:
            written = jnp.concatenate([-weights, updates], 1)
            seen = jnp.concatenate([job["query"], none], 1)
            carried = jnp.concatenate([job["fade"] * eye, none], 1)
        else:
            through = mm(jnp.concatenate([weights, job["query"]], 0), state[h])
            written = jnp.concatenate([none, updates], 1) - through[:SPAN]
            seen = through[SPAN:]
            carried = job["fade"] * state[h]
        readout = seen + mm(job["attend"], written)
        state[h] = carried + mm(job["key_end"], written, ((0,), (0,)))
        slope_ref[h, rows, :] = half(readout[:, :KEY_HEAD_SIZE])
        base_ref[h, rows, :] = readout[:, KEY_HEAD_SIZE:]
    for h in range(ratio):
        maps_ref[h] = state[h]


def block_maps(rim_qk, pre_qk, conv_qk, rim_value, pre_value, conv_value, beta, cumul):
    count = pre_qk.shape[0]
    key_heads = pre_qk.shape[1] // (2 * KEY_HEAD_SIZE)
    heads = pre_value.shape[1] // DV
    ratio = heads // key_heads
    taps = conv_qk.shape[0]
    wide = ratio * DV
    place = (lambda i: (0, i), lambda i: (0, key_heads + i), lambda i: (0, i))
    width = (KEY_HEAD_SIZE, KEY_HEAD_SIZE, wide)
    specs = []
    for at, size in zip(place, width):
        specs += [pl.BlockSpec((tall, size), at) for tall in (EDGE, count, taps)]
    paired = lambda a: jnp.moveaxis(a.reshape(count, key_heads, ratio), 1, 0)
    turned = jnp.moveaxis(cumul.reshape(count, key_heads, ratio), 0, 2)
    whole = lambda i: (i, 0, 0)
    return pl.pallas_call(
        block_kernel,
        grid=(key_heads,),
        in_specs=specs
        + [
            pl.BlockSpec((1, count, ratio), whole),
            pl.BlockSpec((1, count, ratio), whole),
            pl.BlockSpec((1, ratio, count), whole),
        ],
        out_specs=[
            pl.BlockSpec((ratio, KEY_HEAD_SIZE, KEY_HEAD_SIZE + DV), whole),
            pl.BlockSpec((ratio, count, DV), whole),
            pl.BlockSpec((ratio, count, KEY_HEAD_SIZE), whole),
        ],
        out_shape=[
            jax.ShapeDtypeStruct((heads, KEY_HEAD_SIZE, KEY_HEAD_SIZE + DV), jnp.float32),
            jax.ShapeDtypeStruct((heads, count, DV), jnp.float32),
            jax.ShapeDtypeStruct((heads, count, KEY_HEAD_SIZE), jnp.bfloat16),
        ],
        scratch_shapes=[pltpu.VMEM((EDGE + count, wide), jnp.float32)],
    )(
        rim_qk, pre_qk, conv_qk, rim_qk, pre_qk, conv_qk, rim_value, pre_value, conv_value,
        paired(beta), paired(cumul), turned,
    )


def finish_kernel(base_ref, slope_ref, state_ref, gate_ref, gain_ref, w_ref, out_ref):
    pieces = []
    for h in range(base_ref.shape[0]):
        gate = gate_ref[:, h * DV : (h + 1) * DV].astype(jnp.float32)
        output = base_ref[h] + mm(slope_ref[h], state_ref[h])
        scale = lax.rsqrt(jnp.mean(output * output, axis=-1, keepdims=True) + 1e-06)
        pieces.append(half(output * scale * gain_ref[...] * silu(gate)))
    normed = jnp.concatenate(pieces, 1)
    wide = out_ref.shape[2]
    for g in range(out_ref.shape[0]):
        out_ref[g] = half(mm(normed, w_ref[:, g * wide : (g + 1) * wide]))


def finish(base, slope, state, gate_z, norm_gain, w_out, groups):
    count, model_width = gate_z.shape[0], w_out.shape[1]
    return pl.pallas_call(
        finish_kernel,
        out_shape=jax.ShapeDtypeStruct((groups, count, model_width // groups), jnp.bfloat16),
    )(base, slope, state, gate_z, norm_gain.reshape(1, -1), w_out)


def local(
    hidden_in,
    w_qk,
    w_value,
    w_outgate,
    w_ba,
    conv_qk,
    conv_value,
    hist_qk,
    hist_value,
    a_log,
    dt_bias,
    beta_bias,
    state_in,
    norm_gain,
    w_out,
):
    num_rows, model_width = hidden_in.shape
    key_cols = w_qk.shape[2]
    heads = a_log.shape[0]
    taps = conv_value.shape[0]
    leading = lax.axis_index("seq") == 0
    edge_rows = shifted(hidden_in[num_rows - EDGE :], "seq", 1)
    qk_flat = w_qk.reshape(model_width, 2 * key_cols)
    pre_qk = stored(jnp.dot(hidden_in, qk_flat, preferred_element_type=jnp.float32))
    pre_value = stored(jnp.dot(hidden_in, w_value, preferred_element_type=jnp.float32))
    rim_qk = stored(jnp.dot(edge_rows, qk_flat, preferred_element_type=jnp.float32))
    rim_value = stored(jnp.dot(edge_rows, w_value, preferred_element_type=jnp.float32))
    pad = ((EDGE - (taps - 1), 0), (0, 0))
    rim_qk = jnp.where(leading, jnp.pad(hist_qk.reshape(taps - 1, 2 * key_cols), pad), rim_qk)
    rim_value = jnp.where(leading, jnp.pad(hist_value, pad), rim_value)
    gates_in = (
        stored(
            jnp.dot(
                hidden_in, w_ba.reshape(model_width, 2 * heads), preferred_element_type=jnp.float32
            )
        )
        .astype(jnp.float32)
        .reshape(num_rows, 2, heads)
    )
    strength = jax.nn.sigmoid(gates_in[:, 0] + beta_bias)
    log_decay = -jnp.exp(a_log) * jax.nn.softplus(gates_in[:, 1] + dt_bias)
    tokens = jnp.arange(num_rows)
    before = jnp.logical_and(
        tokens[:, None] >= tokens[None, :], tokens[:, None] // SPAN == tokens[None, :] // SPAN
    ).astype(jnp.float32)
    cumul = jnp.dot(before, log_decay, precision=exact_setting)
    maps, base, slope = block_maps(
        rim_qk, pre_qk, conv_qk.reshape(taps, 2 * key_cols),
        rim_value, pre_value, conv_value, strength, cumul,
    )
    carry_map = maps[..., :KEY_HEAD_SIZE]
    carry_add = maps[..., KEY_HEAD_SIZE:]
    gate_z = stored(jnp.dot(hidden_in, w_outgate, preferred_element_type=jnp.float32))
    span_add = jnp.where(leading, mat_batch(carry_map, state_in) + carry_add, carry_add)
    span_map = jnp.where(leading, 0.0, carry_map)
    count = lax.axis_size("seq")
    reach = 1
    while 2 * reach < count:
        both = jnp.concatenate([span_map, span_add], -1).astype(jnp.bfloat16)
        came = shifted(both, "seq", reach).astype(jnp.float32)
        joined = mat_batch(span_map, came)
        has_left = lax.axis_index("seq") >= reach
        span_add = joined[..., KEY_HEAD_SIZE:] + span_add
        span_map = jnp.where(has_left, joined[..., :KEY_HEAD_SIZE], span_map)
        reach = reach * 2
    came = shifted(span_add.astype(jnp.bfloat16), "seq", reach).astype(jnp.float32)
    span_add = mat_batch(span_map, came) + span_add
    checkpoint = span_add[None]
    came = shifted(span_add.astype(jnp.bfloat16), "seq", 1).astype(jnp.float32)
    initial_state = jnp.where(leading, state_in, came)
    groups = lax.axis_size("head")
    terms = finish(base, slope, initial_state, gate_z, norm_gain, w_out, groups)
    terms = lax.all_to_all(terms, "head", 0, 0, tiled=False)
    mixed = jnp.sum(terms.astype(jnp.float32), axis=0).astype(jnp.bfloat16)
    return (mixed, checkpoint)


def solution(mesh):
    return jax.shard_map(
        local,
        mesh=mesh,
        in_specs=(
            P("seq", None),
            P(None, None, "head"),
            P(None, "head"),
            P(None, "head"),
            P(None, None, "head"),
            P(None, None, "head"),
            P(None, "head"),
            P(None, None, "head"),
            P(None, "head"),
            P("head"),
            P("head"),
            P("head"),
            P("head", None, None),
            P(),
            P("head", None),
        ),
        out_specs=(P("seq", "head"), P("seq", "head", None, None)),
        check_vma=False,
    )
```

time: 190 us -> 138 us (0.73)
  matrix products: 53.9 us -> 14.3 us
  local copies, waits for them, and re-layouts: 20.5 us -> 8.28 us
  Pallas kernels: 0 us -> 12.2 us
  other arithmetic: 17.1 us -> 5.39 us
    dot_general x32 -> x3, matrix products: 42.2 us -> 1 us  [the longest x1 0.37 us: local(): jnp.dot(edge_rows, w_value, preferred_element_type=jnp.float32)]
    pallas_call x0 -> x2, Pallas kernels: none -> 12.2 us  [the longest x1 8.2 us: block_maps(): pl.pallas_call(block_kernel, grid=(key_heads,), in_specs=specs + [pl.Bloc...]
    mul x4 -> x0, other arithmetic: 4.59 us -> none  [the longest x2 2.28 us: causal_filter(): return jax.nn.silu(total)]
    reshape x5 -> x0, local copies, waits for them, and re-layouts: 3.79 us -> none  [the longest x1 2.02 us: local(): causal_filter(prev_value, pre_value, conv_value)]
    transpose x4 -> x0, local copies, waits for them, and re-layouts: 3.5 us -> none  [the longest x1 1.32 us: local(): jnp.moveaxis(readout_rows, 0, 1)]
    mul x7 -> x0, local copies, waits for them, and re-layouts: 2.81 us -> none  [the longest x4 2.69 us: advance(): fade[:, None, None] * current_state]
    convert_element_type x4 -> x0, other arithmetic: 2.1 us -> none  [the longest x1 1.88 us: causal_filter(): joined = jnp.concatenate([history, present], 0).astype(jnp.float32)]
    transpose x3 -> x1, other arithmetic: 2.75 us -> 0.79 us  [block_maps(): paired = lambda a: jnp.moveaxis(a.reshape(count, key_heads, ratio), 1, 0)]
  transfers between devices with their start and end apart: 7 -> 7, of which waited for: 6 -> 6; matrix products, arithmetic and copies ran while one was open for 9% -> 8% of each run, Pallas kernels for 0% -> 0%
where the time goes in v2:
time: 138 us
  waiting for transfers between devices  57.4 us (42%)
  blocking collectives  23.1 us (17%)
  starting transfers between devices  15.8 us (11%)
  matrix products  14.3 us (10%)
  Pallas kernels  12.2 us (9%)
  local copies, waits for them, and re-layouts  8.28 us (6%)
  other arithmetic  5.39 us (4%)
    ppermute x7, waiting for transfers between devices, shifted(): lax.ppermute(value, axis, [(source, source + steps) for source in range(l...  57.4 us
    all_to_all x1, blocking collectives, local(): terms = lax.all_to_all(terms, 'head', 0, 0, tiled=False)  23.1 us
    ppermute x7, starting transfers between devices, shifted(): lax.ppermute(value, axis, [(source, source + steps) for source in range(l...  15.8 us
    pallas_call x1, Pallas kernels, block_maps(): pl.pallas_call(block_kernel, grid=(key_heads,), in_specs=specs + [pl.Bloc...  8.2 us
    dot_general x6, matrix products, mat_batch(): return jnp.einsum('hij,hjk->hik', left, right, precision=exact_setting)  6.76 us
    unnamed x35, local copies, waits for them, and re-layouts  6.19 us
    pallas_call x1, Pallas kernels, finish(): pl.pallas_call(finish_kernel, out_shape=jax.ShapeDtypeStruct((groups, cou...  4.05 us
    dot_general x1, matrix products, local(): jnp.dot(hidden_in, w_outgate, preferred_element_type=jnp.float32)  3.32 us
  transfers between devices with their start and end apart: 7, of which 6 were waited for; matrix products, arithmetic and copies ran while one was open for 8% of the time, Pallas kernels for 0%

profile of v2, /device:TPU:7, one launch (start us, length us, event | category | flops | bytes accessed | tf_op | source)
XLA Modules:
  0.0 137.5 jit_solution(13402267779746944108)
XLA Ops:
  0.6 0.0 copy-start
  0.6 0.9 slice.39
  1.6 3.5 %collective-permute-start = (bf16[8,2048]{1,0:T(8,128)(2,1)S(1)}, bf16[8,2048]{1,0:T(8,128)(2,1)S(1)}, u32[]{:S(2)}, u32[]{:S(2)}) collective-permute-start(bf16[8,2048]{1,0:T(8,128)(2,1)S(1)} %slice.39), channel_id=1, source_target_pairs={{0,8},{8,16},{16,24},{24,32},{32,40},{40,48},{48,56},{56,64},{64,7... | collective-permute-start | bytes 98312 | tf_op jit(solution)/shard_map/ppermute | solution.py:34
  5.1 0.0 copy-start.5
  5.1 2.1 %copy.33 = bf16[256,8,2,256]{3,1,2,0:T(8,128)(2,1)S(1)} copy(bf16[256,8,2,256]{3,2,1,0:T(2,128)(2,1)} %bitcast.53) | data formatting | bytes 4194304
  7.3 0.0 copy-start.1
  7.3 1.3 copy-done.1
  8.6 0.0 copy-done.5
  8.6 1.4 %convolution_convert_fusion.2.q_new.k_new = bf16[256,512]{1,0:T(8,128)(2,1)} fusion(bf16[256,2048]{1,0:T(8,128)(2,1)S(1)} %copy-done.5, bf16[2048,512]{1,0:T(8,128)(2,1)S(1)} %bitcast.51), kind=kOutput, calls=%fused_computation.2 | convolution fusion | flops 537001984 | bytes 3407872 | tf_op jit(solution)/shard_map/dot_general | solution.py:230
  10.0 0.0 copy-done
  10.0 0.0 copy-start.13
  10.0 0.0 copy-start.12
  10.0 0.0 copy-start.10
  10.0 1.4 %convolution_convert_fusion.1.v_new = bf16[256,512]{1,0:T(8,128)(2,1)} fusion(bf16[256,2048]{1,0:T(8,128)(2,1)S(1)} %copy-done.5, bf16[2048,512]{1,0:T(8,128)(2,1)S(1)} %copy-done), kind=kOutput, calls=%fused_computation.1 | convolution fusion | flops 537001984 | bytes 3407872 | tf_op jit(solution)/shard_map/dot_general | solution.py:231
  11.4 0.0 copy-done.8
  11.5 0.4 convolution_convert_fusion.5
  11.9 0.2 copy.24
  12.1 0.1 add.61
  12.1 0.1 fusion.16
  12.3 0.8 divide_bitcast_fusion.beta_ref
  13.0 0.3 fusion.3
  13.3 0.1 copy-done.12
  13.4 0.6 copy.34
  14.0 0.9 copy.27
  14.9 0.0 collective-permute-done
  14.9 0.4 convolution_convert_fusion.3
  15.3 1.2 copy-done.2
  16.5 0.4 convolution_convert_fusion.4
  16.8 0.0 copy-done.11
  16.8 0.6 pad_select_fusion
  17.5 8.2 %shard_map.158 = (f32[4,128,256]{2,1,0:T(8,128)}, f32[4,256,128]{2,1,0:T(8,128)}, bf16[4,256,128]{2,1,0:T(8,128)(2,1)}) custom-call(bf16[8,512]{1,0:T(8,128)(2,1)} %get-tuple-element.25.q_rim.k_rim, bf16[256,512]{1,0:T(8,128)(2,1)} %convolution_convert_fusion.2.q_new.k_new, bf16[4,512]{1,0:T(4,128)(2,1)} %bitcast.56, ...), custom_call_target="tpu_custom_call" | custom-call | tf_op jit(solution)/shard_map/pallas_call | solution.py:159
  25.7 1.0 fusion.7
  26.7 0.0 copy-done.6
  26.7 1.4 %fusion.24 = (bf16[4,128,128]{2,1,0:T(8,128)(2,1)S(1)}, f32[4,128,128]{2,1,0:T(8,128)S(1)}) fusion(f32[4,128,256]{2,1,0:T(8,128)} %get-tuple-element.7, f32[4,128,128]{2,1,0:T(8,128)S(1)} %copy-done.6, pred[]{:T(512)S(6)} %eq.16), kind=kOutput, calls=%fused_computation.56 | convolution fusion | flops 100859904 | bytes 1179649 | tf_op jit(solution)/shard_map/hij,hjk->hik/dot_general | solution.py:42
  28.1 3.6 %collective-permute-start.1 = (bf16[4,128,256]{2,1,0:T(8,128)(2,1)S(1)}, bf16[4,128,256]{2,1,0:T(8,128)(2,1)S(1)}, u32[]{:S(2)}, u32[]{:S(2)}) collective-permute-start(bf16[4,128,256]{2,1,0:T(8,128)(2,1)S(1)} %pad_maximum_fusion), channel_id=1, source_target_pairs={{0,8},{8,16},{16,24},{24,32},{32,40},{40,48},{48,56},{56,64},{64,7... | collective-permute-start | bytes 786440 | tf_op jit(solution)/shard_map/ppermute | solution.py:34
  31.7 8.6 %collective-permute-done.1 = bf16[4,128,256]{2,1,0:T(8,128)(2,1)S(1)} collective-permute-done((bf16[4,128,256]{2,1,0:T(8,128)(2,1)S(1)}, bf16[4,128,256]{2,1,0:T(8,128)(2,1)S(1)}, u32[]{:S(2)}, u32[]{:S(2)}) %collective-permute-start.1) | collective-permute-done | bytes 262176 | tf_op jit(solution)/shard_map/ppermute | solution.py:34
  40.3 1.3 fusion.6
  41.6 1.0 fusion.23
  42.6 0.0 copy-start.3
  42.7 2.1 %collective-permute-start.2 = (bf16[4,128,256]{2,1,0:T(8,128)(2,1)S(1)}, bf16[4,128,256]{2,1,0:T(8,128)(2,1)}, u32[]{:S(2)}, u32[]{:S(2)}) collective-permute-start(bf16[4,128,256]{2,1,0:T(8,128)(2,1)S(1)} %pad_maximum_fusion.1), channel_id=1, source_target_pairs={{0,16},{8,24},{16,32},{24,40},{32,48},{40,56},{48,64},{56,72},{64,... | collective-permute-start | bytes 786440 | tf_op jit(solution)/shard_map/ppermute | solution.py:34
  44.9 14.4 %collective-permute-done.2 = bf16[4,128,256]{2,1,0:T(8,128)(2,1)} collective-permute-done((bf16[4,128,256]{2,1,0:T(8,128)(2,1)S(1)}, bf16[4,128,256]{2,1,0:T(8,128)(2,1)}, u32[]{:S(2)}, u32[]{:S(2)}) %collective-permute-start.2) | collective-permute-done | bytes 262176 | tf_op jit(solution)/shard_map/ppermute | solution.py:34
  59.2 0.0 copy-done.3
  59.2 1.3 fusion.26
  60.5 0.1 fusion.21
  60.7 1.9 %collective-permute-start.3 = (bf16[4,128,256]{2,1,0:T(8,128)(2,1)S(1)}, bf16[4,128,256]{2,1,0:T(8,128)(2,1)S(1)}, u32[]{:S(2)}, u32[]{:S(2)}) collective-permute-start(bf16[4,128,256]{2,1,0:T(8,128)(2,1)S(1)} %pad_maximum_fusion.2), channel_id=1, source_target_pairs={{0,32},{8,40},{16,48},{24,56},{32,64},{40,72},{48,80},{56,88},{64,... | collective-permute-start | bytes 786440 | tf_op jit(solution)/shard_map/ppermute | solution.py:34
  62.6 18.0 %collective-permute-done.3 = bf16[4,128,256]{2,1,0:T(8,128)(2,1)S(1)} collective-permute-done((bf16[4,128,256]{2,1,0:T(8,128)(2,1)S(1)}, bf16[4,128,256]{2,1,0:T(8,128)(2,1)S(1)}, u32[]{:S(2)}, u32[]{:S(2)}) %collective-permute-start.3) | collective-permute-done | bytes 262176 | tf_op jit(solution)/shard_map/ppermute | solution.py:34
  80.7 0.4 fusion.27
  81.0 0.1 fusion.20
  81.1 1.3 collective-permute-start.4
  82.4 8.0 %collective-permute-done.4 = bf16[4,128,256]{2,1,0:T(8,128)(2,1)S(1)} collective-permute-done((bf16[4,128,256]{2,1,0:T(8,128)(2,1)S(1)}, bf16[4,128,256]{2,1,0:T(8,128)(2,1)S(1)}, u32[]{:S(2)}, u32[]{:S(2)}) %collective-permute-start.4) | collective-permute-done | bytes 262176 | tf_op jit(solution)/shard_map/ppermute | solution.py:34
  90.4 0.4 fusion.28
  90.8 0.0 copy-start.4
  90.8 0.8 copy-done.4
  91.6 0.1 fusion.19
  91.7 1.3 collective-permute-start.5
  93.0 5.9 %collective-permute-done.5 = bf16[4,128,128]{2,1,0:T(8,128)(2,1)S(1)} collective-permute-done((bf16[4,128,128]{2,1,0:T(8,128)(2,1)S(1)}, bf16[4,128,128]{2,1,0:T(8,128)(2,1)S(1)}, u32[]{:S(2)}, u32[]{:S(2)}) %collective-permute-start.5) | collective-permute-done | bytes 131104 | tf_op jit(solution)/shard_map/ppermute | solution.py:34
  98.9 2.0 %fusion.25 = (bf16[4,128,128]{2,1,0:T(8,128)(2,1)S(1)}, f32[4,128,128]{2,1,0:T(8,128)}) fusion(f32[4,128,128]{2,1,0:T(8,128)S(1)} %get-tuple-element.18, f32[4,128,256]{2,1,0:T(8,128)S(1)} %fusion.27, f32[4,128,256]{2,1,0:T(8,128)} %copy-done.4, bf16[4,128,128]{2,1,0:T(8,128)(2,1)S(1)} %collective-permute-done.5, f32[4,128,128]{2,1,0:T(8,128)S(1)} %get-tuple-element.9, ...), kind=kOutput, calls=%fused_computation.57 | convolution fusion | flops 100990976 | bytes 1835009 | tf_op jit(solution)/shard_map/hij,hjk->hik/dot_general | solution.py:42
  100.9 2.0 %collective-permute-start.6 = (bf16[4,128,128]{2,1,0:T(8,128)(2,1)S(1)}, bf16[4,128,128]{2,1,0:T(8,128)(2,1)S(1)}, u32[]{:S(2)}, u32[]{:S(2)}) collective-permute-start(bf16[4,128,128]{2,1,0:T(8,128)(2,1)S(1)} %get-tuple-element.22), channel_id=1, source_target_pairs={{0,8},{8,16},{16,24},{24,32},{32,40},{40,48},{48,56},{56,64},{64,7... | collective-permute-start | bytes 393224 | tf_op jit(solution)/shard_map/ppermute | solution.py:34
  102.9 3.3 %convolution_convert_fusion.gate_ref = bf16[256,512]{1,0:T(8,128)(2,1)} fusion(bf16[256,2048]{1,0:T(8,128)(2,1)} %param.15, bf16[2048,512]{1,0:T(8,128)(2,1)} %param.18), kind=kOutput, calls=%fused_computation | convolution fusion | flops 537001984 | bytes 3407872 | tf_op jit(solution)/shard_map/dot_general | solution.py:259
  106.2 2.6 %collective-permute-done.6 = bf16[4,128,128]{2,1,0:T(8,128)(2,1)S(1)} collective-permute-done((bf16[4,128,128]{2,1,0:T(8,128)(2,1)S(1)}, bf16[4,128,128]{2,1,0:T(8,128)(2,1)S(1)}, u32[]{:S(2)}, u32[]{:S(2)}) %collective-permute-start.6) | collective-permute-done | bytes 131104 | tf_op jit(solution)/shard_map/ppermute | solution.py:34
  108.8 0.7 convert_select_fusion.state_ref
  109.5 4.1 %shard_map.159 = bf16[8,256,256]{2,1,0:T(8,128)(2,1)} custom-call(f32[4,256,128]{2,1,0:T(8,128)} %get-tuple-element.5.base_ref, bf16[4,256,128]{2,1,0:T(8,128)(2,1)} %get-tuple-element.6.slope_ref, f32[4,128,128]{2,1,0:T(8,128)} %convert_select_fusion.state_ref, bf16[256,512]{1,0:T(8,128)(2,1)} %convolution_convert_fusion.gate_ref, f32[1,128]{1,0:T(1,128)} %bitcast.62, ...), custom_call_target="tpu_custom_call" | custom-call | tf_op jit(solution)/shard_map/pallas_call | solution.py:200
  113.6 23.1 %all_to_all.5 = bf16[8,256,256]{2,1,0:T(8,128)(2,1)S(1)} all-to-all(bf16[8,256,256]{2,1,0:T(8,128)(2,1)} %shard_map.159), channel_id=1, replica_groups=mesh['seq'=32,'head'=8] {'head'}, dimensions={0} | all-to-all | bytes 2097152 | tf_op jit(solution)/shard_map/all_to_all | solution.py:279
  136.7 0.8 reduce_sum.12
  (26 shorter events, 0.2 us)
Async XLA Ops:
  0.6 9.4 %copy-start = (bf16[2048,512]{1,0:T(8,128)(2,1)S(1)}, bf16[2048,512]{1,0:T(8,128)(2,1)}, u32[]{:S(2)}) copy-start(bf16[2048,512]{1,0:T(8,128)(2,1)} %param.17) | copy-start | bytes 6291460
  1.6 13.3 %collective-permute-start = (bf16[8,2048]{1,0:T(8,128)(2,1)S(1)}, bf16[8,2048]{1,0:T(8,128)(2,1)S(1)}, u32[]{:S(2)}, u32[]{:S(2)}) collective-permute-start(bf16[8,2048]{1,0:T(8,128)(2,1)S(1)} %slice.39), channel_id=1, source_target_pairs={{0,8},{8,16},{16,24},{24,32},{32,40},{40,48},{48,56},{56,64},{64,7... | collective-permute-start | bytes 98312 | tf_op jit(solution)/shard_map/ppermute | solution.py:34
  5.1 3.5 %copy-start.5 = (bf16[256,2048]{1,0:T(8,128)(2,1)S(1)}, bf16[256,2048]{1,0:T(8,128)(2,1)}, u32[]{:S(2)}) copy-start(bf16[256,2048]{1,0:T(8,128)(2,1)} %param.15) | copy-start | bytes 3145732
  7.3 1.3 copy-start.1
  10.0 1.4 %copy-start.8 = (bf16[2048,2,4]{0,2,1:T(4,128)(2,1)S(1)}, bf16[2048,2,4]{0,2,1:T(4,128)(2,1)}, u32[]{:S(2)}) copy-start(bf16[2048,2,4]{0,2,1:T(4,128)(2,1)} %param.19) | copy-start | bytes 98308
  10.0 2.0 %copy-start.14 = (f32[4]{0:T(128)S(1)}, f32[4]{0:T(128)}, u32[]{:S(2)}) copy-start(f32[4]{0:T(128)} %param.26) | copy-start | bytes 52
  10.0 2.1 %copy-start.15 = (f32[4]{0:T(128)S(1)}, f32[4]{0:T(128)}, u32[]{:S(2)}) copy-start(f32[4]{0:T(128)} %param.24) | copy-start | bytes 52
  10.0 2.1 %copy-start.13 = (f32[4]{0:T(128)S(1)}, f32[4]{0:T(128)}, u32[]{:S(2)}) copy-start(f32[4]{0:T(128)} %param.25) | copy-start | bytes 52
  10.0 3.4 %copy-start.12 = (bf16[3,2,256]{2,1,0:T(2,128)(2,1)S(1)}, bf16[3,2,256]{2,1,0:T(2,128)(2,1)}, u32[]{:S(2)}) copy-start(bf16[3,2,256]{2,1,0:T(2,128)(2,1)} %param.22) | copy-start | bytes 9220
  10.0 3.4 %copy-start.10 = (bf16[4,2,256]{2,1,0:T(2,128)(2,1)S(1)}, bf16[4,2,256]{2,1,0:T(2,128)(2,1)}, u32[]{:S(2)}) copy-start(bf16[4,2,256]{2,1,0:T(2,128)(2,1)} %param.20) | copy-start | bytes 12292
  13.3 3.5 %copy-start.9 = (f32[256,2,2]{0,2,1:T(2,128)}, f32[256,2,2]{0,2,1:T(2,128)S(1)}, u32[]{:S(2)}) copy-start(f32[256,2,2]{0,2,1:T(2,128)S(1)} %fusion.3) | copy-start | bytes 12292
  14.9 1.6 %copy-start.2 = (bf16[256,8,2,256]{3,1,2,0:T(8,128)(2,1)S(1)}, bf16[256,8,2,256]{3,1,2,0:T(8,128)(2,1)}, u32[]{:S(2)}) copy-start(bf16[256,8,2,256]{3,1,2,0:T(8,128)(2,1)} %copy-done.1) | copy-start | bytes 6291460
  14.9 2.0 %copy-start.11 = (bf16[3,512]{1,0:T(4,128)(2,1)S(1)}, bf16[3,512]{1,0:T(4,128)(2,1)}, u32[]{:S(2)}) copy-start(bf16[3,512]{1,0:T(4,128)(2,1)} %param.23) | copy-start | bytes 9220
  16.5 10.2 %copy-start.6 = (f32[4,128,128]{2,1,0:T(8,128)S(1)}, f32[4,128,128]{2,1,0:T(8,128)}, u32[]{:S(2)}) copy-start(f32[4,128,128]{2,1,0:T(8,128)} %param.27) | copy-start | bytes 786436
  28.1 12.2 %collective-permute-start.1 = (bf16[4,128,256]{2,1,0:T(8,128)(2,1)S(1)}, bf16[4,128,256]{2,1,0:T(8,128)(2,1)S(1)}, u32[]{:S(2)}, u32[]{:S(2)}) collective-permute-start(bf16[4,128,256]{2,1,0:T(8,128)(2,1)S(1)} %pad_maximum_fusion), channel_id=1, source_target_pairs={{0,8},{8,16},{16,24},{24,32},{32,40},{40,48},{48,56},{56,64},{64,7... | collective-permute-start | bytes 786440 | tf_op jit(solution)/shard_map/ppermute | solution.py:34
  42.6 16.6 %copy-start.3 = (f32[4,128,128]{2,1,0:T(8,128)}, f32[4,128,128]{2,1,0:T(8,128)S(1)}, u32[]{:S(2)}) copy-start(f32[4,128,128]{2,1,0:T(8,128)S(1)} %get-tuple-element.15) | copy-start | bytes 786436
  42.7 16.5 %collective-permute-start.2 = (bf16[4,128,256]{2,1,0:T(8,128)(2,1)S(1)}, bf16[4,128,256]{2,1,0:T(8,128)(2,1)}, u32[]{:S(2)}, u32[]{:S(2)}) collective-permute-start(bf16[4,128,256]{2,1,0:T(8,128)(2,1)S(1)} %pad_maximum_fusion.1), channel_id=1, source_target_pairs={{0,16},{8,24},{16,32},{24,40},{32,48},{40,56},{48,64},{56,72},{64,... | collective-permute-start | bytes 786440 | tf_op jit(solution)/shard_map/ppermute | solution.py:34
  60.7 20.0 %collective-permute-start.3 = (bf16[4,128,256]{2,1,0:T(8,128)(2,1)S(1)}, bf16[4,128,256]{2,1,0:T(8,128)(2,1)S(1)}, u32[]{:S(2)}, u32[]{:S(2)}) collective-permute-start(bf16[4,128,256]{2,1,0:T(8,128)(2,1)S(1)} %pad_maximum_fusion.2), channel_id=1, source_target_pairs={{0,32},{8,40},{16,48},{24,56},{32,64},{40,72},{48,80},{56,88},{64,... | collective-permute-start | bytes 786440 | tf_op jit(solution)/shard_map/ppermute | solution.py:34
  81.1 9.3 %collective-permute-start.4 = (bf16[4,128,256]{2,1,0:T(8,128)(2,1)S(1)}, bf16[4,128,256]{2,1,0:T(8,128)(2,1)S(1)}, u32[]{:S(2)}, u32[]{:S(2)}) collective-permute-start(bf16[4,128,256]{2,1,0:T(8,128)(2,1)S(1)} %pad_maximum_fusion.3), channel_id=1, source_target_pairs={{0,64},{8,72},{16,80},{24,88},{32,96},{40,104},{48,112},{56,120},{... | collective-permute-start | bytes 786440 | tf_op jit(solution)/shard_map/ppermute | solution.py:34
  90.8 0.8 copy-start.4
  91.7 7.2 %collective-permute-start.5 = (bf16[4,128,128]{2,1,0:T(8,128)(2,1)S(1)}, bf16[4,128,128]{2,1,0:T(8,128)(2,1)S(1)}, u32[]{:S(2)}, u32[]{:S(2)}) collective-permute-start(bf16[4,128,128]{2,1,0:T(8,128)(2,1)S(1)} %fusion.19), channel_id=1, source_target_pairs={{0,128},{8,136},{16,144},{24,152},{32,160},{40,168},{48,176},{56,1... | collective-permute-start | bytes 393224 | tf_op jit(solution)/shard_map/ppermute | solution.py:34
  100.9 7.9 %copy-start.7 = (f32[4,128,128]{2,1,0:T(8,128)S(1)}, f32[4,128,128]{2,1,0:T(8,128)}, u32[]{:S(2)}) copy-start(f32[4,128,128]{2,1,0:T(8,128)} %param.27) | copy-start | bytes 786436
  100.9 7.9 %collective-permute-start.6 = (bf16[4,128,128]{2,1,0:T(8,128)(2,1)S(1)}, bf16[4,128,128]{2,1,0:T(8,128)(2,1)S(1)}, u32[]{:S(2)}, u32[]{:S(2)}) collective-permute-start(bf16[4,128,128]{2,1,0:T(8,128)(2,1)S(1)} %get-tuple-element.22), channel_id=1, source_target_pairs={{0,8},{8,16},{16,24},{24,32},{32,40},{40,48},{48,56},{56,64},{64,7... | collective-permute-start | bytes 393224 | tf_op jit(solution)/shard_map/ppermute | solution.py:34

commit v3 on v2

--- a/solution.py
+++ b/solution.py
@@ -36,10 +36,6 @@
 
 def stored(values):
     return lax.optimization_barrier(values.astype(jnp.bfloat16))
-
-
-def mat_batch(left, right):
-    return jnp.einsum("hij,hjk->hik", left, right, precision=exact_setting)
 
 
 def filtered(rim_ref, present_ref, weight_ref, room):
@@ -182,25 +178,203 @@
     )
 
 
-def finish_kernel(base_ref, slope_ref, state_ref, gate_ref, gain_ref, w_ref, out_ref):
+def carry_kernel(
+    maps_ref, base_ref, slope_ref, start_ref, gate_ref, gain_ref, w_ref, mixed_ref, check_ref,
+    parts, gathered, before, states, hop_out, hop_in, terms, landed,
+    part_send, part_recv, back_send, back_recv, hop_send, hop_recv, term_send, term_recv,
+    *, count, groups,
+):
+    heads = maps_ref.shape[0]
+    row = parts.shape[0]
+    lines = count // row
+    cut = row // heads
+    tall = DV // cut
+    place = lax.axis_index("seq")
+    group = lax.axis_index("head")
+    unit = lax.rem(place, row)
+    line = place // row
+    first = place - unit
+    mesh_id = pl.DeviceIdType.MESH
+
+    def mate(off):
+        return lax.rem(unit + off, row)
+
+    def peer(off):
+        return lax.rem(group + off, groups)
+
+    barrier = pltpu.get_barrier_semaphore()
+    for off in range(1, row):
+        pl.semaphore_signal(
+            barrier, inc=1, device_id={"seq": first + mate(off)}, device_id_type=mesh_id
+        )
+    for step in (row, count - row):
+        pl.semaphore_signal(
+            barrier, inc=1, device_id={"seq": lax.rem(place + step, count)}, device_id_type=mesh_id
+        )
+    for off in range(1, groups):
+        pl.semaphore_signal(barrier, inc=1, device_id={"head": peer(off)}, device_id_type=mesh_id)
+
+    for h in range(heads):
+        carry_map = half(maps_ref[h, :, :KEY_HEAD_SIZE])
+        carry_add = half(maps_ref[h, :, KEY_HEAD_SIZE:].T)
+        for c in range(cut):
+            parts[h * cut + c, :KEY_HEAD_SIZE, :] = carry_map
+            parts[h * cut + c, KEY_HEAD_SIZE:, :] = carry_add[c * tall : (c + 1) * tall]
+    pl.semaphore_wait(barrier, (row - 1) + 2 + (groups - 1))
+
+    def part_copy(off):
+        return pltpu.make_async_remote_copy(
+            src_ref=parts.at[mate(off)],
+            dst_ref=gathered.at[unit],
+            send_sem=part_send.at[off],
+            recv_sem=part_recv.at[off],
+            device_id={"seq": first + mate(off)},
+            device_id_type=mesh_id,
+        )
+
+    moving = [part_copy(off) for off in range(1, row)]
+    for copy in moving:
+        copy.start()
+    gathered[unit] = parts[unit]
+    for h in range(heads):
+        turned = start_ref[h].T
+        for c in range(cut):
+
+            @pl.when(unit == h * cut + c)
+            def _():
+                hop_out[...] = turned[c * tall : (c + 1) * tall]
+
+    for copy in moving:
+        copy.wait()
+
+    hop = pltpu.make_async_remote_copy(
+        src_ref=hop_out,
+        dst_ref=hop_in,
+        send_sem=hop_send,
+        recv_sem=hop_recv,
+        device_id={"seq": lax.rem(place + row, count)},
+        device_id_type=mesh_id,
+    )
+
+    @pl.when(line > 0)
+    def _():
+        hop.wait_recv()
+        hop_out[...] = hop_in[...]
+
+    state = hop_out[...]
+    for n in range(row):
+        top = half(state)
+        before[n] = top
+        rest = half(state - top.astype(jnp.float32))
+        both = mm(
+            jnp.concatenate([top, rest], 0), gathered[n, :KEY_HEAD_SIZE, :], ((1,), (1,))
+        )
+        state = both[:tall] + both[tall:] + gathered[n, KEY_HEAD_SIZE:, :].astype(jnp.float32)
+    hop_out[...] = state
+
+    @pl.when(line < lines - 1)
+    def _():
+        hop.start()
+
+    returning = [
+        pltpu.make_async_remote_copy(
+            src_ref=before.at[mate(off)],
+            dst_ref=states.at[unit],
+            send_sem=back_send.at[off],
+            recv_sem=back_recv.at[off],
+            device_id={"seq": first + mate(off)},
+            device_id_type=mesh_id,
+        )
+        for off in range(1, row)
+    ]
+    for copy in returning:
+        copy.start()
+    states[unit] = before[unit]
+    for copy in returning:
+        copy.wait()
+
     pieces = []
-    for h in range(base_ref.shape[0]):
+    for h in range(heads):
+        turned = jnp.concatenate([states[h * cut + c] for c in range(cut)], 0)
         gate = gate_ref[:, h * DV : (h + 1) * DV].astype(jnp.float32)
-        output = base_ref[h] + mm(slope_ref[h], state_ref[h])
+        output = base_ref[h] + mm(slope_ref[h], turned, ((1,), (1,)))
         scale = lax.rsqrt(jnp.mean(output * output, axis=-1, keepdims=True) + 1e-06)
         pieces.append(half(output * scale * gain_ref[...] * silu(gate)))
     normed = jnp.concatenate(pieces, 1)
-    wide = out_ref.shape[2]
-    for g in range(out_ref.shape[0]):
-        out_ref[g] = half(mm(normed, w_ref[:, g * wide : (g + 1) * wide]))
-
-
-def finish(base, slope, state, gate_z, norm_gain, w_out, groups):
-    count, model_width = gate_z.shape[0], w_out.shape[1]
+    wide = mixed_ref.shape[1]
+
+    def term(where):
+        columns = pl.ds(pl.multiple_of(where * wide, wide), wide)
+        return half(mm(normed, w_ref[:, columns]))
+
+    leaving = []
+    for off in range(1, groups):
+        terms[off] = term(peer(off))
+        copy = pltpu.make_async_remote_copy(
+            src_ref=terms.at[off],
+            dst_ref=landed.at[off],
+            send_sem=term_send.at[off],
+            recv_sem=term_recv.at[off],
+            device_id={"head": peer(off)},
+            device_id_type=mesh_id,
+        )
+        copy.start()
+        leaving.append(copy)
+    total = term(group).astype(jnp.float32)
+    for h in range(heads):
+        turned = jnp.concatenate([states[h * cut + c] for c in range(cut)], 0)
+        check_ref[h] = (
+            mm(maps_ref[h, :, :KEY_HEAD_SIZE], turned, ((1,), (1,)))
+            + maps_ref[h, :, KEY_HEAD_SIZE:]
+        )
+    for off, copy in enumerate(leaving, 1):
+        copy.wait()
+        total = total + landed[off].astype(jnp.float32)
+    mixed_ref[...] = half(total)
+
+    @pl.when(line < lines - 1)
+    def _():
+        hop.wait_send()
+
+
+def carry(maps, base, slope, state_in, gate_z, norm_gain, w_out):
+    rows, model_width = gate_z.shape[0], w_out.shape[1]
+    heads = maps.shape[0]
+    count, groups = lax.axis_size("seq"), lax.axis_size("head")
+    unit_count = min(2 * heads, count)
+    tall = DV * heads // unit_count
+    wide = model_width // groups
+    dma = pltpu.SemaphoreType.DMA
     return pl.pallas_call(
-        finish_kernel,
-        out_shape=jax.ShapeDtypeStruct((groups, count, model_width // groups), jnp.bfloat16),
-    )(base, slope, state, gate_z, norm_gain.reshape(1, -1), w_out)
+        functools.partial(carry_kernel, count=count, groups=groups),
+        out_shape=[
+            jax.ShapeDtypeStruct((rows, wide), jnp.bfloat16),
+            jax.ShapeDtypeStruct((heads, KEY_HEAD_SIZE, DV), jnp.float32),
+        ],
+        in_specs=[pl.BlockSpec(memory_space=pltpu.VMEM)] * 7,
+        out_specs=[pl.BlockSpec(memory_space=pltpu.VMEM)] * 2,
+        scratch_shapes=[
+            pltpu.VMEM((unit_count, KEY_HEAD_SIZE + tall, KEY_HEAD_SIZE), jnp.bfloat16),
+            pltpu.VMEM((unit_count, KEY_HEAD_SIZE + tall, KEY_HEAD_SIZE), jnp.bfloat16),
+            pltpu.VMEM((unit_count, tall, KEY_HEAD_SIZE), jnp.bfloat16),
+            pltpu.VMEM((unit_count, tall, KEY_HEAD_SIZE), jnp.bfloat16),
+            pltpu.VMEM((tall, KEY_HEAD_SIZE), jnp.float32),
+            pltpu.VMEM((tall, KEY_HEAD_SIZE), jnp.float32),
+            pltpu.VMEM((groups, rows, wide), jnp.bfloat16),
+            pltpu.VMEM((groups, rows, wide), jnp.bfloat16),
+            dma((unit_count,)),
+            dma((unit_count,)),
+            dma((unit_count,)),
+            dma((unit_count,)),
+            dma(()),
+            dma(()),
+            dma((groups,)),
+            dma((groups,)),
+        ],
+        compiler_params=pltpu.CompilerParams(
+            collective_id=0, has_side_effects=True, vmem_limit_bytes=40 * 2**20
+        ),
+    )(maps, base, slope, state_in, gate_z, norm_gain.reshape(1, -1), w_out)
 
 
 def local(
@@ -254,31 +428,9 @@
         rim_qk, pre_qk, conv_qk.reshape(taps, 2 * key_cols),
         rim_value, pre_value, conv_value, strength, cumul,
     )
-    carry_map = maps[..., :KEY_HEAD_SIZE]
-    carry_add = maps[..., KEY_HEAD_SIZE:]
     gate_z = stored(jnp.dot(hidden_in, w_outgate, preferred_element_type=jnp.float32))
-    span_add = jnp.where(leading, mat_batch(carry_map, state_in) + carry_add, carry_add)
-    span_map = jnp.where(leading, 0.0, carry_map)
-    count = lax.axis_size("seq")
-    reach = 1
-    while 2 * reach < count:
-        both = jnp.concatenate([span_map, span_add], -1).astype(jnp.bfloat16)
-        came = shifted(both, "seq", reach).astype(jnp.float32)
-        joined = mat_batch(span_map, came)
-        has_left = lax.axis_index("seq") >= reach
-        span_add = joined[..., KEY_HEAD_SIZE:] + span_add
-        span_map = jnp.where(has_left, joined[..., :KEY_HEAD_SIZE], span_map)
-        reach = reach * 2
-    came = shifted(span_add.astype(jnp.bfloat16), "seq", reach).astype(jnp.float32)
-    span_add = mat_batch(span_map, came) + span_add
-    checkpoint = span_add[None]
-    came = shifted(span_add.astype(jnp.bfloat16), "seq", 1).astype(jnp.float32)
-    initial_state = jnp.where(leading, state_in, came)
-    groups = lax.axis_size("head")
-    terms = finish(base, slope, initial_state, gate_z, norm_gain, w_out, groups)
-    terms = lax.all_to_all(terms, "head", 0, 0, tiled=False)
-    mixed = jnp.sum(terms.astype(jnp.float32), axis=0).astype(jnp.bfloat16)
-    return (mixed, checkpoint)
+    mixed, checkpoint = carry(maps, base, slope, state_in, gate_z, norm_gain, w_out)
+    return (mixed, checkpoint[None])
 
 
 def solution(mesh):

time: 138 us -> 81 us (0.59)
  waiting for transfers between devices: 57.4 us -> 0.01 us
  Pallas kernels: 12.2 us -> 54.1 us
  blocking collectives: 23.1 us -> 0 us
  starting transfers between devices: 15.8 us -> 3.53 us
  matrix products: 14.3 us -> 6.53 us
  local copies, waits for them, and re-layouts: 8.28 us -> 14.2 us
  other arithmetic: 5.39 us -> 1.49 us
    ppermute x7 -> x1, waiting for transfers between devices: 57.4 us -> 0.01 us  [shifted(): lax.ppermute(value, axis, [(source, source + steps) for source in range(l...]
    pallas_call x1, Pallas kernels: 4.05 us -> 45.9 us  [carry(): pl.pallas_call(functools.partial(carry_kernel, count=count, groups=groups...]
    all_to_all x1 -> x0, blocking collectives: 23.1 us -> none  [local(): terms = lax.all_to_all(terms, 'head', 0, 0, tiled=False)]
    ppermute x7 -> x1, starting transfers between devices: 15.8 us -> 3.53 us  [shifted(): lax.ppermute(value, axis, [(source, source + steps) for source in range(l...]
    dot_general x6 -> x0, matrix products: 6.76 us -> none  [mat_batch(): return jnp.einsum('hij,hjk->hik', left, right, precision=exact_setting)]
    unnamed x35 -> x43, local copies, waits for them, and re-layouts: 6.19 us -> 11.3 us
    another operation x4 -> x0, other arithmetic: 2.16 us -> none
  transfers between devices with their start and end apart: 7 -> 1, of which waited for: 6 -> 0; matrix products, arithmetic and copies ran while one was open for 8% -> 14% of each run, Pallas kernels for 0% -> 0%
where the time goes in v3:
time: 81 us; the launch traced here: 80.7 us
  Pallas kernels  54.1 us (67%)
  local copies, waits for them, and re-layouts  14.2 us (18%)
  matrix products  6.53 us (8%)
  starting transfers between devices  3.53 us (4%)
  other arithmetic  1.49 us (2%)
  between operations  0.83 us (1%)
    pallas_call x1, Pallas kernels, carry(): pl.pallas_call(functools.partial(carry_kernel, count=count, groups=groups...  45.9 us
    unnamed x43, local copies, waits for them, and re-layouts  11.3 us
    pallas_call x1, Pallas kernels, block_maps(): pl.pallas_call(block_kernel, grid=(key_heads,), in_specs=specs + [pl.Bloc...  8.21 us
    ppermute x1, starting transfers between devices, shifted(): lax.ppermute(value, axis, [(source, source + steps) for source in range(l...  3.53 us
    dot_general x1, matrix products, local(): jnp.dot(hidden_in, w_outgate, preferred_element_type=jnp.float32)  2.33 us
  transfers between devices with their start and end apart: 1, of which 0 were waited for; matrix products, arithmetic and copies ran while one was open for 14% of the time, Pallas kernels for 0%

profile of v3, /device:TPU:7, one launch (start us, length us, event | category | flops | bytes accessed | tf_op | source)
XLA Modules:
  0.0 80.7 jit_solution(9241957604623845697)
XLA Ops:
  0.6 0.0 copy-start
  0.6 0.9 %slice.9 = bf16[8,2048]{1,0:T(8,128)(2,1)S(1)} slice(bf16[256,2048]{1,0:T(8,128)(2,1)} %param.15), slice={[248:256], [0:2048]} | slice | bytes 65536 | tf_op jit(solution)/shard_map/slice | solution.py:402
  1.6 3.5 %collective-permute-start = (bf16[8,2048]{1,0:T(8,128)(2,1)S(1)}, bf16[8,2048]{1,0:T(8,128)(2,1)S(1)}, u32[]{:S(2)}, u32[]{:S(2)}) collective-permute-start(bf16[8,2048]{1,0:T(8,128)(2,1)S(1)} %slice.9), channel_id=1, source_target_pairs={{0,8},{8,16},{16,24},{24,32},{32,40},{40,48},{48,56},{56,64},{64,7... | collective-permute-start | bytes 98312 | tf_op jit(solution)/shard_map/ppermute | solution.py:34
  5.1 0.0 copy-start.9
  5.1 2.1 %copy.25 = bf16[256,8,2,256]{3,1,2,0:T(8,128)(2,1)S(1)} copy(bf16[256,8,2,256]{3,2,1,0:T(2,128)(2,1)} %bitcast.46) | data formatting | bytes 4194304
  7.3 0.0 copy-start.7
  7.3 1.3 %copy-done.7 = bf16[256,8,2,256]{3,1,2,0:T(8,128)(2,1)} copy-done((bf16[256,8,2,256]{3,1,2,0:T(8,128)(2,1)}, bf16[256,8,2,256]{3,1,2,0:T(8,128)(2,1)S(1)}, u32[]{:S(2)}) %copy-start.7) | copy-done | bytes 2097176
  8.6 0.0 copy-done.9
  8.6 1.4 %convolution_convert_fusion.2.q_new.k_new = bf16[256,512]{1,0:T(8,128)(2,1)} fusion(bf16[256,2048]{1,0:T(8,128)(2,1)S(1)} %copy-done.9, bf16[2048,512]{1,0:T(8,128)(2,1)S(1)} %bitcast.44), kind=kOutput, calls=%fused_computation.2 | convolution fusion | flops 537001984 | bytes 3407872 | tf_op jit(solution)/shard_map/dot_general | solution.py:404
  10.0 0.0 copy-done
  10.0 0.0 copy-start.11
  10.0 0.0 copy-start.17
  10.0 0.0 copy-start.18
  10.0 0.0 copy-start.16
  10.0 1.4 %convolution_convert_fusion.1.v_new = bf16[256,512]{1,0:T(8,128)(2,1)} fusion(bf16[256,2048]{1,0:T(8,128)(2,1)S(1)} %copy-done.9, bf16[2048,512]{1,0:T(8,128)(2,1)S(1)} %copy-done), kind=kOutput, calls=%fused_computation.1 | convolution fusion | flops 537001984 | bytes 3407872 | tf_op jit(solution)/shard_map/dot_general | solution.py:405
  11.4 0.0 copy-done.11
  11.5 0.4 convolution_convert_fusion.5
  11.9 0.9 %copy.20 = f32[256,2,2]{2,0,1:T(8,128)} copy(f32[256,2,2]{0,2,1:T(2,128)S(1)} %squeeze.6) | data formatting | bytes 8192 | tf_op jit(solution)/shard_map/squeeze | solution.py:420
  12.7 0.0 copy-done.17
  12.7 0.1 add.43
  12.8 0.0 copy-done.18
  12.8 0.0 copy-done.16
  12.8 0.1 fusion.7
  12.9 0.0 copy-start.10
  12.9 0.0 copy-start.15
  13.0 0.0 copy-start.13
  13.0 2.3 %convolution_convert_fusion.gate_ref = bf16[256,512]{1,0:T(8,128)(2,1)S(1)} fusion(bf16[256,2048]{1,0:T(8,128)(2,1)S(1)} %copy-done.9, bf16[2048,512]{1,0:T(8,128)(2,1)} %param.18), kind=kOutput, calls=%fused_computation | convolution fusion | flops 537001984 | bytes 3407872 | tf_op jit(solution)/shard_map/dot_general | solution.py:431
  15.3 0.0 copy-done.10
  15.3 0.8 divide_bitcast_fusion.beta_ref
  16.1 0.3 fusion.2
  16.4 0.0 copy-start.12
  16.4 0.1 copy-done.15
  16.4 0.0 copy-done.13
  16.5 0.6 copy.26
  17.0 0.9 %copy.23 = f32[256,2,2]{2,0,1:T(8,128)} copy(f32[256,2,2]{0,2,1:T(2,128)S(1)} %fusion.2) | data formatting | bytes 8192 | tf_op jit(solution)/shard_map/dot_general | solution.py:426
  17.9 0.0 copy-start.8
  17.9 0.0 copy-start.14
  17.9 0.0 collective-permute-done
  17.9 0.4 convolution_convert_fusion.3
  18.3 1.2 %copy-done.8 = bf16[256,8,2,256]{3,1,2,0:T(8,128)(2,1)S(1)} copy-done((bf16[256,8,2,256]{3,1,2,0:T(8,128)(2,1)S(1)}, bf16[256,8,2,256]{3,1,2,0:T(8,128)(2,1)}, u32[]{:S(2)}) %copy-start.8) | copy-done | bytes 2097176
  19.5 0.0 copy-start.4
  19.5 0.0 copy-start.6
  19.5 0.4 convolution_convert_fusion.4
  19.9 0.0 copy-done.12
  19.9 0.0 copy-done.14
  19.9 0.6 pad_select_fusion
  20.5 8.2 %shard_map.158 = (f32[4,128,256]{2,1,0:T(8,128)}, f32[4,256,128]{2,1,0:T(8,128)}, bf16[4,256,128]{2,1,0:T(8,128)(2,1)}) custom-call(bf16[8,512]{1,0:T(8,128)(2,1)} %get-tuple-element.13.q_rim.k_rim, bf16[256,512]{1,0:T(8,128)(2,1)} %convolution_convert_fusion.2.q_new.k_new, bf16[4,512]{1,0:T(4,128)(2,1)} %bitcast.48, ...), custom_call_target="tpu_custom_call" | custom-call | tf_op jit(solution)/shard_map/pallas_call | solution.py:155
  28.7 0.0 copy-done.4
  28.7 0.0 copy-done.6
  28.8 0.0 copy-start.1
  28.8 1.6 %copy-done.1 = bf16[512,2048]{1,0:T(8,128)(2,1)S(1)} copy-done((bf16[512,2048]{1,0:T(8,128)(2,1)S(1)}, bf16[512,2048]{1,0:T(8,128)(2,1)}, u32[]{:S(2)}) %copy-start.1) | copy-done | bytes 2097176
  30.3 0.0 copy-start.2
  30.3 1.0 %copy-done.2 = f32[4,128,256]{2,1,0:T(8,128)S(1)} copy-done((f32[4,128,256]{2,1,0:T(8,128)S(1)}, f32[4,128,256]{2,1,0:T(8,128)}, u32[]{:S(2)}) %copy-start.2) | copy-done | bytes 524312
  31.4 0.0 copy-start.3
  31.4 1.0 %copy-done.3 = f32[4,256,128]{2,1,0:T(8,128)S(1)} copy-done((f32[4,256,128]{2,1,0:T(8,128)S(1)}, f32[4,256,128]{2,1,0:T(8,128)}, u32[]{:S(2)}) %copy-start.3) | copy-done | bytes 524312
  32.4 0.0 copy-start.5
  32.4 0.9 %copy-done.5 = bf16[4,256,128]{2,1,0:T(8,128)(2,1)S(1)} copy-done((bf16[4,256,128]{2,1,0:T(8,128)(2,1)S(1)}, bf16[4,256,128]{2,1,0:T(8,128)(2,1)}, u32[]{:S(2)}) %copy-start.5) | copy-done | bytes 262168
  33.4 45.9 %shard_map.159 = (bf16[256,256]{1,0:T(8,128)(2,1)S(1)}, f32[4,128,128]{2,1,0:T(8,128)S(1)}) custom-call(f32[4,128,256]{2,1,0:T(8,128)S(1)} %copy-done.2, f32[4,256,128]{2,1,0:T(8,128)S(1)} %copy-done.3, bf16[4,256,128]{2,1,0:T(8,128)(2,1)S(1)} %copy-done.5, f32[4,128,128]{2,1,0:T(8,128)S(1)} %copy-done.4, ...), custom_call_target="tpu_custom_call" | custom-call | tf_op jit(solution)/shard_map/pallas_call | solution.py:348
  79.3 0.7 copy.29
  80.0 0.7 copy.30
  (8 shorter events, 0.1 us)
Async XLA Ops:
  0.6 9.4 %copy-start = (bf16[2048,512]{1,0:T(8,128)(2,1)S(1)}, bf16[2048,512]{1,0:T(8,128)(2,1)}, u32[]{:S(2)}) copy-start(bf16[2048,512]{1,0:T(8,128)(2,1)} %param.17) | copy-start | bytes 6291460
  1.6 16.4 %collective-permute-start = (bf16[8,2048]{1,0:T(8,128)(2,1)S(1)}, bf16[8,2048]{1,0:T(8,128)(2,1)S(1)}, u32[]{:S(2)}, u32[]{:S(2)}) collective-permute-start(bf16[8,2048]{1,0:T(8,128)(2,1)S(1)} %slice.9), channel_id=1, source_target_pairs={{0,8},{8,16},{16,24},{24,32},{32,40},{40,48},{48,56},{56,64},{64,7... | collective-permute-start | bytes 98312 | tf_op jit(solution)/shard_map/ppermute | solution.py:34
  5.1 3.5 %copy-start.9 = (bf16[256,2048]{1,0:T(8,128)(2,1)S(1)}, bf16[256,2048]{1,0:T(8,128)(2,1)}, u32[]{:S(2)}) copy-start(bf16[256,2048]{1,0:T(8,128)(2,1)} %param.15) | copy-start | bytes 3145732
  7.3 1.3 %copy-start.7 = (bf16[256,8,2,256]{3,1,2,0:T(8,128)(2,1)}, bf16[256,8,2,256]{3,1,2,0:T(8,128)(2,1)S(1)}, u32[]{:S(2)}) copy-start(bf16[256,8,2,256]{3,1,2,0:T(8,128)(2,1)S(1)} %copy.25) | copy-start | bytes 6291460
  10.0 1.4 %copy-start.11 = (bf16[2048,2,4]{0,2,1:T(4,128)(2,1)S(1)}, bf16[2048,2,4]{0,2,1:T(4,128)(2,1)}, u32[]{:S(2)}) copy-start(bf16[2048,2,4]{0,2,1:T(4,128)(2,1)} %param.19) | copy-start | bytes 98308
  10.0 2.7 %copy-start.17 = (f32[4]{0:T(128)S(1)}, f32[4]{0:T(128)}, u32[]{:S(2)}) copy-start(f32[4]{0:T(128)} %param.26) | copy-start | bytes 52
  10.0 2.8 %copy-start.18 = (f32[4]{0:T(128)S(1)}, f32[4]{0:T(128)}, u32[]{:S(2)}) copy-start(f32[4]{0:T(128)} %param.24) | copy-start | bytes 52
  10.0 2.8 %copy-start.16 = (f32[4]{0:T(128)S(1)}, f32[4]{0:T(128)}, u32[]{:S(2)}) copy-start(f32[4]{0:T(128)} %param.25) | copy-start | bytes 52
  12.9 2.4 %copy-start.10 = (f32[256,2,2]{2,0,1:T(8,128)S(1)}, f32[256,2,2]{2,0,1:T(8,128)}, u32[]{:S(2)}) copy-start(f32[256,2,2]{2,0,1:T(8,128)} %copy.20) | copy-start | bytes 12292
  12.9 3.5 %copy-start.15 = (bf16[3,2,256]{2,1,0:T(2,128)(2,1)S(1)}, bf16[3,2,256]{2,1,0:T(2,128)(2,1)}, u32[]{:S(2)}) copy-start(bf16[3,2,256]{2,1,0:T(2,128)(2,1)} %param.22) | copy-start | bytes 9220
  13.0 3.5 %copy-start.13 = (bf16[4,2,256]{2,1,0:T(2,128)(2,1)S(1)}, bf16[4,2,256]{2,1,0:T(2,128)(2,1)}, u32[]{:S(2)}) copy-start(bf16[4,2,256]{2,1,0:T(2,128)(2,1)} %param.20) | copy-start | bytes 12292
  16.4 3.5 %copy-start.12 = (f32[256,2,2]{0,2,1:T(2,128)}, f32[256,2,2]{0,2,1:T(2,128)S(1)}, u32[]{:S(2)}) copy-start(f32[256,2,2]{0,2,1:T(2,128)S(1)} %fusion.2) | copy-start | bytes 12292
  17.9 1.6 %copy-start.8 = (bf16[256,8,2,256]{3,1,2,0:T(8,128)(2,1)S(1)}, bf16[256,8,2,256]{3,1,2,0:T(8,128)(2,1)}, u32[]{:S(2)}) copy-start(bf16[256,8,2,256]{3,1,2,0:T(8,128)(2,1)} %copy-done.7) | copy-start | bytes 6291460
  17.9 2.0 %copy-start.14 = (bf16[3,512]{1,0:T(4,128)(2,1)S(1)}, bf16[3,512]{1,0:T(4,128)(2,1)}, u32[]{:S(2)}) copy-start(bf16[3,512]{1,0:T(4,128)(2,1)} %param.23) | copy-start | bytes 9220
  19.5 9.2 %copy-start.4 = (f32[4,128,128]{2,1,0:T(8,128)S(1)}, f32[4,128,128]{2,1,0:T(8,128)}, u32[]{:S(2)}) copy-start(f32[4,128,128]{2,1,0:T(8,128)} %start_ref.1) | copy-start | bytes 786436
  19.5 9.2 %copy-start.6 = (f32[128]{0:T(128)S(1)}, f32[128]{0:T(128)}, u32[]{:S(2)}) copy-start(f32[128]{0:T(128)} %param.28) | copy-start | bytes 1540
  28.8 1.6 %copy-start.1 = (bf16[512,2048]{1,0:T(8,128)(2,1)S(1)}, bf16[512,2048]{1,0:T(8,128)(2,1)}, u32[]{:S(2)}) copy-start(bf16[512,2048]{1,0:T(8,128)(2,1)} %w_ref.1) | copy-start | bytes 6291460
  30.3 1.0 %copy-start.2 = (f32[4,128,256]{2,1,0:T(8,128)S(1)}, f32[4,128,256]{2,1,0:T(8,128)}, u32[]{:S(2)}) copy-start(f32[4,128,256]{2,1,0:T(8,128)} %get-tuple-element.7.maps_ref) | copy-start | bytes 1572868
  31.4 1.0 %copy-start.3 = (f32[4,256,128]{2,1,0:T(8,128)S(1)}, f32[4,256,128]{2,1,0:T(8,128)}, u32[]{:S(2)}) copy-start(f32[4,256,128]{2,1,0:T(8,128)} %get-tuple-element.8.base_ref) | copy-start | bytes 1572868
  32.4 0.9 %copy-start.5 = (bf16[4,256,128]{2,1,0:T(8,128)(2,1)S(1)}, bf16[4,256,128]{2,1,0:T(8,128)(2,1)}, u32[]{:S(2)}) copy-start(bf16[4,256,128]{2,1,0:T(8,128)(2,1)} %get-tuple-element.9.slope_ref) | copy-start | bytes 786436

commit v4 on v3

v4 whole, which is shorter than its diff:
```python
import functools

import jax
import jax.numpy as jnp
from jax import lax
from jax.experimental import pallas as pl
from jax.experimental.pallas import tpu as pltpu
from jax.sharding import PartitionSpec as P

KEY_HEAD_SIZE = 128
DV = 128
SPAN = 128
EDGE = 16
LANES = 128


exact_setting = lax.Precision.HIGHEST


def half(values):
    return values.astype(jnp.bfloat16)


def mm(left, right, dims=((1,), (0,))):
    return lax.dot_general(half(left), half(right), (dims, ((), ())), preferred_element_type=jnp.float32)


def silu(values):
    return values / (1.0 + jnp.exp(-values))


def stored(values):
    return lax.optimization_barrier(values.astype(jnp.bfloat16))


def filtered(room, weight_ref, columns, shift, begin, count):
    taps = weight_ref.shape[0]
    first = EDGE - (taps - 1) + begin
    wide = columns.stop - columns.start
    where = slice(columns.start + shift, columns.stop + shift)
    total = jnp.zeros((count, wide), jnp.float32)
    for tap in range(taps):
        weight = weight_ref[tap : tap + 1, columns].astype(jnp.float32)
        total = total + weight * room[first + tap : first + tap + count, where]
    return silu(total)


def unit_rows(values):
    return values * lax.rsqrt(jnp.sum(values * values, axis=-1, keepdims=True) + 1e-06)


def unit_inverses(lowers, row, col):
    size = row.shape[0]
    eye = jnp.where(row == col, 1.0, 0.0)
    step = 1
    results = None
    while step < size:
        pair = jnp.logical_and(row // (2 * step) == col // (2 * step), row // step > col // step)
        cross = [jnp.where(pair, lower, 0.0) for lower in lowers]
        if results is None:
            results = [eye - c for c in cross]
        else:
            inner = [mm(c, x) for c, x in zip(cross, results)]
            results = [x - mm(x, y) for x, y in zip(results, inner)]
        step = 2 * step
    return results


def layer_kernel(
    pre_qk, pre_value, taps_qk, taps_value, history, gates_ref, rows_ref, start_ref, gain_ref,
    hidden_hbm, gate_hbm, out_hbm, mixed_ref, check_ref,
    room, rim_qk, rim_value, maps_ref, base_ref, slope_ref, hidden, w_gate, w_ref,
    parts, gathered, before, states, hop_out, hop_in, terms, landed,
    fetch_sem, rim_send, rim_recv,
    part_send, part_recv, back_send, back_recv, hop_send, hop_recv, term_send, term_recv,
    *, count, groups,
):
    heads = maps_ref.shape[0]
    tokens = pre_qk.shape[0]
    key_cols = pre_qk.shape[1] // 2
    key_heads = key_cols // KEY_HEAD_SIZE
    ratio = heads // key_heads
    row = parts.shape[0]
    lines = count // row
    cut = row // heads
    tall = DV // cut
    place = lax.axis_index("seq")
    group = lax.axis_index("head")
    unit = lax.rem(place, row)
    line = place // row
    first = place - unit
    mesh_id = pl.DeviceIdType.MESH

    def mate(off):
        return lax.rem(unit + off, row)

    def peer(off):
        return lax.rem(group + off, groups)

    barrier = pltpu.get_barrier_semaphore()
    for step in (1, count - 1, row, count - row):
        pl.semaphore_signal(
            barrier, inc=1, device_id={"seq": lax.rem(place + step, count)}, device_id_type=mesh_id
        )
    for off in range(1, row):
        pl.semaphore_signal(
            barrier, inc=1, device_id={"seq": first + mate(off)}, device_id_type=mesh_id
        )
    for off in range(1, groups):
        pl.semaphore_signal(barrier, inc=1, device_id={"head": peer(off)}, device_id_type=mesh_id)

    fetches = [
        pltpu.make_async_copy(source, target, fetch_sem.at[i])
        for i, (source, target) in enumerate(
            ((hidden_hbm, hidden), (gate_hbm, w_gate), (out_hbm, w_ref))
        )
    ]
    for copy in fetches:
        copy.start()

    gates = gates_ref[...].astype(jnp.float32) + rows_ref[0:1, :]
    strength = 1.0 / (1.0 + jnp.exp(-gates))
    soft = jnp.maximum(gates, 0.0) + jnp.log1p(jnp.exp(-jnp.abs(gates)))
    log_decay = -jnp.exp(rows_ref[1:2, :]) * soft
    row_at = lax.broadcasted_iota(jnp.int32, (SPAN, SPAN), 0)
    col_at = lax.broadcasted_iota(jnp.int32, (SPAN, SPAN), 1)
    running = jnp.where(row_at >= col_at, 1.0, 0.0)
    eye = jnp.where(row_at == col_at, 1.0, 0.0)

    pl.semaphore_wait(barrier, 4 + (row - 1) + (groups - 1))
    rims = [
        pltpu.make_async_remote_copy(
            src_ref=source.at[pl.ds(tokens - EDGE, EDGE)],
            dst_ref=target,
            send_sem=rim_send.at[i],
            recv_sem=rim_recv.at[i],
            device_id={"seq": lax.rem(place + 1, count)},
            device_id_type=mesh_id,
        )
        for i, (source, target) in enumerate(((pre_qk, rim_qk), (pre_value, rim_value)))
    ]

    @pl.when(place < count - 1)
    def _():
        for copy in rims:
            copy.start()

    room[EDGE:, : 2 * key_cols] = pre_qk[...].astype(jnp.float32)
    room[EDGE:, 2 * key_cols :] = pre_value[...].astype(jnp.float32)

    def chunk(n):
        begin = n * SPAN
        rows = slice(begin, begin + SPAN)
        cumul_all = jnp.dot(running, log_decay[rows], precision=exact_setting)
        turned_all = cumul_all.T
        jobs = []
        for kh in range(key_heads):
            q_at = slice(kh * KEY_HEAD_SIZE, (kh + 1) * KEY_HEAD_SIZE)
            k_at = slice(key_cols + q_at.start, key_cols + q_at.stop)
            query = unit_rows(filtered(room, taps_qk, q_at, 0, begin, SPAN))
            query = query * KEY_HEAD_SIZE ** (-0.5)
            key = unit_rows(filtered(room, taps_qk, k_at, 0, begin, SPAN))
            key_dots = mm(key, key, ((1,), (1,)))
            query_dots = mm(query, key, ((1,), (1,)))
            for h in range(kh * ratio, (kh + 1) * ratio):
                v_at = slice(h * DV, (h + 1) * DV)
                value = filtered(room, taps_value, v_at, 2 * key_cols, begin, SPAN)
                beta = strength[rows, h : h + 1]
                cumul = cumul_all[:, heads + h : heads + h + 1]
                turned = turned_all[heads + h : heads + h + 1, :]
                last = turned[:, SPAN - 1 :]
                fading = jnp.exp(jnp.where(row_at >= col_at, cumul - turned, 0.0))
                grown = jnp.exp(cumul)
                jobs.append(
                    dict(
                        h=h,
                        lower=jnp.where(row_at > col_at, beta * fading * key_dots, 0.0),
                        attend=half(jnp.where(row_at >= col_at, fading * query_dots, 0.0)),
                        sides=half(jnp.concatenate([beta * grown * key, beta * value], 1)),
                        query=grown * query,
                        key_end=half(jnp.exp(last - cumul) * key),
                        fade=jnp.exp(last),
                    )
                )
        inverses = unit_inverses([job["lower"] for job in jobs], row_at, col_at)
        for job, inverse in zip(jobs, inverses):
            job["both"] = mm(inverse, job["sides"])
        return jobs

    blocks = tokens // SPAN
    prepared = {n: chunk(n) for n in range(1, blocks)}

    @pl.when(place > 0)
    def _():
        for copy in rims:
            copy.wait_recv()
        room[:EDGE, : 2 * key_cols] = rim_qk[...].astype(jnp.float32)
        room[:EDGE, 2 * key_cols :] = rim_value[...].astype(jnp.float32)

    @pl.when(place == 0)
    def _():
        room[:EDGE, :] = history[...].astype(jnp.float32)

    prepared[0] = chunk(0)
    none = jnp.zeros((SPAN, DV), jnp.float32)
    state = [None] * heads
    for n in range(blocks):
        rows = slice(n * SPAN, (n + 1) * SPAN)
        for job in prepared[n]:
            h, both = job["h"], job["both"]
            weights, updates = both[:, :KEY_HEAD_SIZE], both[:, KEY_HEAD_SIZE:]
            if n == 0:
                written = jnp.concatenate([-weights, updates], 1)
                seen = jnp.concatenate([job["query"], none], 1)
                carried = jnp.concatenate([job["fade"] * eye, none], 1)
            else:
                through = mm(jnp.concatenate([weights, job["query"]], 0), state[h])
                written = jnp.concatenate([none, updates], 1) - through[:SPAN]
                seen = through[SPAN:]
                carried = job["fade"] * state[h]
            readout = seen + mm(job["attend"], written)
            state[h] = carried + mm(job["key_end"], written, ((0,), (0,)))
            slope_ref[h, rows, :] = half(readout[:, :KEY_HEAD_SIZE])
            base_ref[h, rows, :] = readout[:, KEY_HEAD_SIZE:]
    for h in range(heads):
        maps_ref[h] = state[h]

    for h in range(heads):
        carry_map = half(maps_ref[h, :, :KEY_HEAD_SIZE])
        carry_add = half(maps_ref[h, :, KEY_HEAD_SIZE:].T)
        for c in range(cut):
            parts[h * cut + c, :KEY_HEAD_SIZE, :] = carry_map
            parts[h * cut + c, KEY_HEAD_SIZE:, :] = carry_add[c * tall : (c + 1) * tall]
    def part_copy(off):
        return pltpu.make_async_remote_copy(
            src_ref=parts.at[mate(off)],
            dst_ref=gathered.at[unit],
            send_sem=part_send.at[off],
            recv_sem=part_recv.at[off],
            device_id={"seq": first + mate(off)},
            device_id_type=mesh_id,
        )

    moving = [part_copy(off) for off in range(1, row)]
    for copy in moving:
        copy.start()
    gathered[unit] = parts[unit]
    for h in range(heads):
        turned = start_ref[h].T
        for c in range(cut):

            @pl.when(unit == h * cut + c)
            def _():
                hop_out[...] = turned[c * tall : (c + 1) * tall]

    for copy in fetches:
        copy.wait()
    gate_all = half(mm(hidden[...], w_gate[...])).astype(jnp.float32)
    for copy in moving:
        copy.wait()

    hop = pltpu.make_async_remote_copy(
        src_ref=hop_out,
        dst_ref=hop_in,
        send_sem=hop_send,
        recv_sem=hop_recv,
        device_id={"seq": lax.rem(place + row, count)},
        device_id_type=mesh_id,
    )

    @pl.when(line > 0)
    def _():
        hop.wait_recv()
        hop_out[...] = hop_in[...]

    state = hop_out[...]
    for n in range(row):
        top = half(state)
        before[n] = top
        rest = half(state - top.astype(jnp.float32))
        both = mm(
            jnp.concatenate([top, rest], 0), gathered[n, :KEY_HEAD_SIZE, :], ((1,), (1,))
        )
        state = both[:tall] + both[tall:] + gathered[n, KEY_HEAD_SIZE:, :].astype(jnp.float32)
    hop_out[...] = state

    @pl.when(line < lines - 1)
    def _():
        hop.start()

    returning = [
        pltpu.make_async_remote_copy(
            src_ref=before.at[mate(off)],
            dst_ref=states.at[unit],
            send_sem=back_send.at[off],
            recv_sem=back_recv.at[off],
            device_id={"seq": first + mate(off)},
            device_id_type=mesh_id,
        )
        for off in range(1, row)
    ]
    for copy in returning:
        copy.start()
    states[unit] = before[unit]
    for copy in returning:
        copy.wait()

    pieces = []
    for h in range(heads):
        turned = jnp.concatenate([states[h * cut + c] for c in range(cut)], 0)
        gate = gate_all[:, h * DV : (h + 1) * DV]
        output = base_ref[h] + mm(slope_ref[h], turned, ((1,), (1,)))
        scale = lax.rsqrt(jnp.mean(output * output, axis=-1, keepdims=True) + 1e-06)
        pieces.append(half(output * scale * gain_ref[...] * silu(gate)))
    normed = jnp.concatenate(pieces, 1)
    wide = mixed_ref.shape[1]

    def term(where):
        columns = pl.ds(pl.multiple_of(where * wide, wide), wide)
        return half(mm(normed, w_ref[:, columns]))

    leaving = []
    for off in range(1, groups):
        terms[off] = term(peer(off))
        copy = pltpu.make_async_remote_copy(
            src_ref=terms.at[off],
            dst_ref=landed.at[off],
            send_sem=term_send.at[off],
            recv_sem=term_recv.at[off],
            device_id={"head": peer(off)},
            device_id_type=mesh_id,
        )
        copy.start()
        leaving.append(copy)
    total = term(group).astype(jnp.float32)
    for h in range(heads):
        turned = jnp.concatenate([states[h * cut + c] for c in range(cut)], 0)
        check_ref[h] = (
            mm(maps_ref[h, :, :KEY_HEAD_SIZE], turned, ((1,), (1,)))
            + maps_ref[h, :, KEY_HEAD_SIZE:]
        )
    for off, copy in enumerate(leaving, 1):
        copy.wait()
        total = total + landed[off].astype(jnp.float32)
    mixed_ref[...] = half(total)

    @pl.when(line < lines - 1)
    def _():
        hop.wait_send()

    @pl.when(place < count - 1)
    def _():
        for copy in rims:
            copy.wait_send()


def layer(
    pre_qk, pre_value, taps_qk, taps_value, history, gates, rows, state_in, gain,
    hidden, w_gate, w_out,
):
    tokens, model_width = hidden.shape
    heads = state_in.shape[0]
    count, groups = lax.axis_size("seq"), lax.axis_size("head")
    unit_count = min(2 * heads, count)
    tall = DV * heads // unit_count
    wide = model_width // groups
    room_wide = pre_qk.shape[1] + pre_value.shape[1]
    dma = pltpu.SemaphoreType.DMA
    bf16, f32 = jnp.bfloat16, jnp.float32
    return pl.pallas_call(
        functools.partial(layer_kernel, count=count, groups=groups),
        out_shape=[
            jax.ShapeDtypeStruct((tokens, wide), bf16),
            jax.ShapeDtypeStruct((heads, KEY_HEAD_SIZE, DV), f32),
        ],
        in_specs=[pl.BlockSpec(memory_space=pltpu.VMEM)] * 9
        + [pl.BlockSpec(memory_space=pl.ANY)] * 3,
        out_specs=[pl.BlockSpec(memory_space=pltpu.VMEM)] * 2,
        scratch_shapes=[
            pltpu.VMEM((EDGE + tokens, room_wide), f32),
            pltpu.VMEM((EDGE, pre_qk.shape[1]), bf16),
            pltpu.VMEM((EDGE, pre_value.shape[1]), bf16),
            pltpu.VMEM((heads, KEY_HEAD_SIZE, KEY_HEAD_SIZE + DV), f32),
            pltpu.VMEM((heads, tokens, DV), f32),
            pltpu.VMEM((heads, tokens, KEY_HEAD_SIZE), bf16),
            pltpu.VMEM(hidden.shape, bf16),
            pltpu.VMEM(w_gate.shape, bf16),
            pltpu.VMEM(w_out.shape, bf16),
            pltpu.VMEM((unit_count, KEY_HEAD_SIZE + tall, KEY_HEAD_SIZE), bf16),
            pltpu.VMEM((unit_count, KEY_HEAD_SIZE + tall, KEY_HEAD_SIZE), bf16),
            pltpu.VMEM((unit_count, tall, KEY_HEAD_SIZE), bf16),
            pltpu.VMEM((unit_count, tall, KEY_HEAD_SIZE), bf16),
            pltpu.VMEM((tall, KEY_HEAD_SIZE), f32),
            pltpu.VMEM((tall, KEY_HEAD_SIZE), f32),
            pltpu.VMEM((groups, tokens, wide), bf16),
            pltpu.VMEM((groups, tokens, wide), bf16),
            dma((3,)),
            dma((2,)),
            dma((2,)),
            dma((unit_count,)),
            dma((unit_count,)),
            dma((unit_count,)),
            dma((unit_count,)),
            dma(()),
            dma(()),
            dma((groups,)),
            dma((groups,)),
        ],
        compiler_params=pltpu.CompilerParams(
            collective_id=0, has_side_effects=True, vmem_limit_bytes=40 * 2**20
        ),
    )(
        pre_qk, pre_value, taps_qk, taps_value, history, gates, rows, state_in, gain,
        hidden, w_gate, w_out,
    )


def local(
    hidden_in,
    w_qk,
    w_value,
    w_outgate,
    w_ba,
    conv_qk,
    conv_value,
    hist_qk,
    hist_value,
    a_log,
    dt_bias,
    beta_bias,
    state_in,
    norm_gain,
    w_out,
):
    num_rows, model_width = hidden_in.shape
    key_cols = w_qk.shape[2]
    heads = a_log.shape[0]
    taps = conv_value.shape[0]
    qk_flat = w_qk.reshape(model_width, 2 * key_cols)
    pre_qk = stored(jnp.dot(hidden_in, qk_flat, preferred_element_type=jnp.float32))
    pre_value = stored(jnp.dot(hidden_in, w_value, preferred_element_type=jnp.float32))
    w_gates = jnp.pad(w_ba.reshape(model_width, 2 * heads), ((0, 0), (0, LANES - 2 * heads)))
    gates = stored(jnp.dot(hidden_in, w_gates, preferred_element_type=jnp.float32))
    history = jnp.concatenate([hist_qk.reshape(taps - 1, 2 * key_cols), hist_value], 1)
    history = jnp.pad(history, ((EDGE - (taps - 1), 0), (0, 0)))
    unused = jnp.zeros((LANES - 2 * heads,), jnp.float32)
    rows = jnp.stack(
        [
            jnp.concatenate([beta_bias, dt_bias, unused]),
            jnp.concatenate([a_log, a_log, unused]),
        ]
    )
    mixed, checkpoint = layer(
        pre_qk, pre_value, conv_qk.reshape(taps, 2 * key_cols), conv_value, history, gates, rows,
        state_in, norm_gain.reshape(1, -1), hidden_in, w_outgate, w_out,
    )
    return (mixed, checkpoint[None])


def solution(mesh):
    return jax.shard_map(
        local,
        mesh=mesh,
        in_specs=(
            P("seq", None),
            P(None, None, "head"),
            P(None, "head"),
            P(None, "head"),
            P(None, None, "head"),
            P(None, None, "head"),
            P(None, "head"),
            P(None, None, "head"),
            P(None, "head"),
            P("head"),
            P("head"),
            P("head"),
            P("head", None, None),
            P(),
            P("head", None),
        ),
        out_specs=(P("seq", "head"), P("seq", "head", None, None)),
        check_vma=False,
    )
```

time: 81 us -> 68 us (0.84)
  local copies, waits for them, and re-layouts: 14.2 us -> 8.73 us
  starting transfers between devices: 3.53 us -> 0 us
  matrix products: 6.53 us -> 3.21 us
  other arithmetic: 1.49 us -> 0.1 us
    ppermute x1 -> x0, starting transfers between devices: 3.53 us -> none  [shifted(): lax.ppermute(value, axis, [(source, source + steps) for source in range(l...]
    dot_general x5 -> x1, matrix products: 3.7 us -> 0.4 us  [local(): jnp.dot(hidden_in, w_gates, preferred_element_type=jnp.float32)]
    unnamed x43 -> x37, local copies, waits for them, and re-layouts: 11.3 us -> 8.71 us
    slice x2 -> x0, local copies, waits for them, and re-layouts: 0.92 us -> none  [the longest x1 0.91 us: local(): edge_rows = shifted(hidden_in[num_rows - EDGE:], 'seq', 1)]
    dot_general x2 -> x0, local copies, waits for them, and re-layouts: 0.89 us -> none  [local(): cumul = jnp.dot(before, log_decay, precision=exact_setting)]
    squeeze x2 -> x0, local copies, waits for them, and re-layouts: 0.89 us -> none  [local(): strength = jax.nn.sigmoid(gates_in[:, 0] + beta_bias)]
    pallas_call x2 -> x1, Pallas kernels: 54.1 us -> 54.9 us  [layer(): pl.pallas_call(functools.partial(layer_kernel, count=count, groups=groups...]
  transfers between devices with their start and end apart: 1 -> 0, of which waited for: 0 -> 0; matrix products, arithmetic and copies ran while one was open for 14% -> 0% of each run, Pallas kernels for 0% -> 0%
where the time goes in v4:
time: 68 us; the launch traced here: 67.8 us
  Pallas kernels  54.9 us (81%)
  local copies, waits for them, and re-layouts  8.73 us (13%)
  matrix products  3.21 us (5%)
  between operations  0.84 us (1%)
    pallas_call x1, Pallas kernels, layer(): pl.pallas_call(functools.partial(layer_kernel, count=count, groups=groups...  54.9 us
    unnamed x37, local copies, waits for them, and re-layouts  8.71 us
    dot_general x1, matrix products, local(): jnp.dot(hidden_in, qk_flat, preferred_element_type=jnp.float32)  1.41 us
    dot_general x1, matrix products, local(): jnp.dot(hidden_in, w_value, preferred_element_type=jnp.float32)  1.4 us

profile of v4, /device:TPU:7, one launch (start us, length us, event | category | flops | bytes accessed | tf_op | source)
XLA Modules:
  0.0 67.8 jit_solution(17933733808513661990)
XLA Ops:
  0.6 0.0 copy-start
  0.6 0.0 copy-start.3
  0.7 2.2 %copy.19 = bf16[256,8,2,256]{3,1,2,0:T(8,128)(2,1)S(1)} copy(bf16[256,8,2,256]{3,2,1,0:T(2,128)(2,1)} %bitcast.24) | data formatting | bytes 4194304
  2.9 0.0 copy-done.3
  2.9 1.4 %convolution_convert_fusion.1.pre_qk = bf16[256,512]{1,0:T(8,128)(2,1)} fusion(bf16[256,2048]{1,0:T(8,128)(2,1)S(1)} %copy-done.3, bf16[2048,512]{1,0:T(8,128)(2,1)S(1)} %bitcast.25), kind=kOutput, calls=%fused_computation.1 | convolution fusion | flops 537001984 | bytes 3407872 | tf_op jit(solution)/shard_map/dot_general | solution.py:440
  4.3 0.0 copy-done
  4.3 0.0 copy-start.11
  4.3 0.0 copy-start.12
  4.3 0.0 copy-start.10
  4.3 0.0 copy-start.9
  4.3 0.0 copy-start.13
  4.3 0.0 copy-start.14
  4.3 0.0 copy-start.15
  4.3 0.0 copy-start.4
  4.4 0.0 copy-start.7
  4.4 0.0 copy-start.8
  4.4 1.4 %convolution_convert_fusion.pre_value = bf16[256,512]{1,0:T(8,128)(2,1)} fusion(bf16[256,2048]{1,0:T(8,128)(2,1)S(1)} %copy-done.3, bf16[2048,512]{1,0:T(8,128)(2,1)S(1)} %copy-done), kind=kOutput, calls=%fused_computation | convolution fusion | flops 537001984 | bytes 3407872 | tf_op jit(solution)/shard_map/dot_general | solution.py:441
  5.8 0.0 copy-done.11
  5.8 0.0 copy-done.12
  5.8 0.0 copy-done.10
  5.8 0.0 copy-done.9
  5.9 0.4 fusion.gates_ref
  6.3 0.0 copy-done.13
  6.3 0.0 copy-done.14
  6.3 0.0 copy-done.15
  6.3 0.1 fusion.5
  6.4 0.0 copy-done.4
  6.4 0.0 copy-done.7
  6.4 0.0 copy-done.8
  6.4 0.0 copy-start.1
  6.4 1.6 %copy-done.1 = bf16[2048,512]{1,0:T(8,128)(2,1)S(1)} copy-done((bf16[2048,512]{1,0:T(8,128)(2,1)S(1)}, bf16[2048,512]{1,0:T(8,128)(2,1)}, u32[]{:S(2)}) %copy-start.1) | copy-done | bytes 2097176
  8.0 0.0 copy-start.2
  8.0 1.6 %copy-done.2 = bf16[512,2048]{1,0:T(8,128)(2,1)S(1)} copy-done((bf16[512,2048]{1,0:T(8,128)(2,1)S(1)}, bf16[512,2048]{1,0:T(8,128)(2,1)}, u32[]{:S(2)}) %copy-start.2) | copy-done | bytes 2097176
  9.6 0.0 copy-start.5
  9.6 0.9 %copy-done.5 = bf16[256,512]{1,0:T(8,128)(2,1)S(1)} copy-done((bf16[256,512]{1,0:T(8,128)(2,1)S(1)}, bf16[256,512]{1,0:T(8,128)(2,1)}, u32[]{:S(2)}) %copy-start.5) | copy-done | bytes 262168
  10.6 0.0 copy-start.6
  10.6 0.9 %copy-done.6 = bf16[256,512]{1,0:T(8,128)(2,1)S(1)} copy-done((bf16[256,512]{1,0:T(8,128)(2,1)S(1)}, bf16[256,512]{1,0:T(8,128)(2,1)}, u32[]{:S(2)}) %copy-start.6) | copy-done | bytes 262168
  11.5 54.9 %shard_map.158 = (bf16[256,256]{1,0:T(8,128)(2,1)S(1)}, f32[4,128,128]{2,1,0:T(8,128)S(1)}) custom-call(bf16[256,512]{1,0:T(8,128)(2,1)S(1)} %copy-done.5, bf16[256,512]{1,0:T(8,128)(2,1)S(1)} %copy-done.6, bf16[4,512]{1,0:T(4,128)(2,1)S(1)} %bitcast.22, bf16[4,512]{1,0:T(4,128)(2,1)S(1)} %copy-done.7, bf16[16,1024]{1,0:T(8,128)(2,1)S(1)} %fusion.4.history, ...), custom_call_target="tpu_custom_call" | custom-call | tf_op jit(solution)/shard_map/pallas_call | solution.py:370
  66.5 0.7 copy.24
  67.1 0.7 %copy.25 = f32[1,4,128,128]{3,2,1,0:T(8,128)} copy(f32[1,4,128,128]{3,2,1,0:T(8,128)S(1)} %bitcast.21) | data formatting | bytes 524288
  (6 shorter events, 0.1 us)
Async XLA Ops:
  0.6 3.7 %copy-start = (bf16[2048,512]{1,0:T(8,128)(2,1)S(1)}, bf16[2048,512]{1,0:T(8,128)(2,1)}, u32[]{:S(2)}) copy-start(bf16[2048,512]{1,0:T(8,128)(2,1)} %param.17) | copy-start | bytes 6291460
  0.6 2.2 %copy-start.3 = (bf16[256,2048]{1,0:T(8,128)(2,1)S(1)}, bf16[256,2048]{1,0:T(8,128)(2,1)}, u32[]{:S(2)}) copy-start(bf16[256,2048]{1,0:T(8,128)(2,1)} %hidden_hbm.1) | copy-start | bytes 3145732
  4.3 1.5 %copy-start.11 = (bf16[4,2,256]{2,1,0:T(2,128)(2,1)S(1)}, bf16[4,2,256]{2,1,0:T(2,128)(2,1)}, u32[]{:S(2)}) copy-start(bf16[4,2,256]{2,1,0:T(2,128)(2,1)} %param.20) | copy-start | bytes 12292
  4.3 1.5 %copy-start.12 = (bf16[3,2,256]{2,1,0:T(2,128)(2,1)S(1)}, bf16[3,2,256]{2,1,0:T(2,128)(2,1)}, u32[]{:S(2)}) copy-start(bf16[3,2,256]{2,1,0:T(2,128)(2,1)} %param.22) | copy-start | bytes 9220
  4.3 1.5 %copy-start.10 = (bf16[3,512]{1,0:T(4,128)(2,1)S(1)}, bf16[3,512]{1,0:T(4,128)(2,1)}, u32[]{:S(2)}) copy-start(bf16[3,512]{1,0:T(4,128)(2,1)} %param.23) | copy-start | bytes 9220
  4.3 1.5 %copy-start.9 = (bf16[2048,2,4]{0,2,1:T(4,128)(2,1)S(1)}, bf16[2048,2,4]{0,2,1:T(4,128)(2,1)}, u32[]{:S(2)}) copy-start(bf16[2048,2,4]{0,2,1:T(4,128)(2,1)} %param.19) | copy-start | bytes 98308
  4.3 2.0 %copy-start.13 = (f32[4]{0:T(128)S(1)}, f32[4]{0:T(128)}, u32[]{:S(2)}) copy-start(f32[4]{0:T(128)} %param.25) | copy-start | bytes 52
  4.3 2.0 %copy-start.14 = (f32[4]{0:T(128)S(1)}, f32[4]{0:T(128)}, u32[]{:S(2)}) copy-start(f32[4]{0:T(128)} %param.26) | copy-start | bytes 52
  4.3 2.0 %copy-start.15 = (f32[4]{0:T(128)S(1)}, f32[4]{0:T(128)}, u32[]{:S(2)}) copy-start(f32[4]{0:T(128)} %param.24) | copy-start | bytes 52
  4.3 2.1 %copy-start.4 = (f32[4,128,128]{2,1,0:T(8,128)S(1)}, f32[4,128,128]{2,1,0:T(8,128)}, u32[]{:S(2)}) copy-start(f32[4,128,128]{2,1,0:T(8,128)} %start_ref.1) | copy-start | bytes 786436
  4.4 2.1 %copy-start.7 = (bf16[4,512]{1,0:T(4,128)(2,1)S(1)}, bf16[4,512]{1,0:T(4,128)(2,1)}, u32[]{:S(2)}) copy-start(bf16[4,512]{1,0:T(4,128)(2,1)} %taps_value.1) | copy-start | bytes 12292
  4.4 2.1 %copy-start.8 = (f32[128]{0:T(128)S(1)}, f32[128]{0:T(128)}, u32[]{:S(2)}) copy-start(f32[128]{0:T(128)} %param.28) | copy-start | bytes 1540
  6.4 1.6 %copy-start.1 = (bf16[2048,512]{1,0:T(8,128)(2,1)S(1)}, bf16[2048,512]{1,0:T(8,128)(2,1)}, u32[]{:S(2)}) copy-start(bf16[2048,512]{1,0:T(8,128)(2,1)} %gate_hbm.1) | copy-start | bytes 6291460
  8.0 1.6 %copy-start.2 = (bf16[512,2048]{1,0:T(8,128)(2,1)S(1)}, bf16[512,2048]{1,0:T(8,128)(2,1)}, u32[]{:S(2)}) copy-start(bf16[512,2048]{1,0:T(8,128)(2,1)} %out_hbm.1) | copy-start | bytes 6291460
  9.6 0.9 %copy-start.5 = (bf16[256,512]{1,0:T(8,128)(2,1)S(1)}, bf16[256,512]{1,0:T(8,128)(2,1)}, u32[]{:S(2)}) copy-start(bf16[256,512]{1,0:T(8,128)(2,1)} %convolution_convert_fusion.1.pre_qk) | copy-start | bytes 786436
  10.6 0.9 %copy-start.6 = (bf16[256,512]{1,0:T(8,128)(2,1)S(1)}, bf16[256,512]{1,0:T(8,128)(2,1)}, u32[]{:S(2)}) copy-start(bf16[256,512]{1,0:T(8,128)(2,1)} %convolution_convert_fusion.pre_value) | copy-start | bytes 786436

commit v5 on v4

--- a/solution.py
+++ b/solution.py
@@ -70,7 +70,7 @@
     pre_qk, pre_value, taps_qk, taps_value, history, gates_ref, rows_ref, start_ref, gain_ref,
     hidden_hbm, gate_hbm, out_hbm, mixed_ref, check_ref,
     room, rim_qk, rim_value, maps_ref, base_ref, slope_ref, hidden, w_gate, w_ref,
-    parts, gathered, before, states, hop_out, hop_in, terms, landed,
+    parts, gathered, before, states, entry, hop_out, hop_in, terms, landed,
     fetch_sem, rim_send, rim_recv,
     part_send, part_recv, back_send, back_recv, hop_send, hop_recv, term_send, term_recv,
     *, count, groups,
@@ -251,7 +251,7 @@
 
             @pl.when(unit == h * cut + c)
             def _():
-                hop_out[...] = turned[c * tall : (c + 1) * tall]
+                entry[...] = turned[c * tall : (c + 1) * tall]
 
     for copy in fetches:
         copy.wait()
@@ -268,25 +268,57 @@
         device_id_type=mesh_id,
     )
 
-    @pl.when(line > 0)
-    def _():
-        hop.wait_recv()
-        hop_out[...] = hop_in[...]
-
-    state = hop_out[...]
-    for n in range(row):
-        top = half(state)
-        before[n] = top
-        rest = half(state - top.astype(jnp.float32))
+    def onward(values, n):
+        top = half(values)
+        rest = half(values - top.astype(jnp.float32))
         both = mm(
             jnp.concatenate([top, rest], 0), gathered[n, :KEY_HEAD_SIZE, :], ((1,), (1,))
         )
-        state = both[:tall] + both[tall:] + gathered[n, KEY_HEAD_SIZE:, :].astype(jnp.float32)
-    hop_out[...] = state
-
-    @pl.when(line < lines - 1)
-    def _():
-        hop.start()
+        return both[: values.shape[0]] + both[values.shape[0] :]
+
+    def added(n):
+        return gathered[n, KEY_HEAD_SIZE:, :].astype(jnp.float32)
+
+    @pl.when(line > 0)
+    def _():
+        blank = jnp.zeros((KEY_HEAD_SIZE, KEY_HEAD_SIZE), jnp.float32)
+        sweep = jnp.concatenate([eye, jnp.zeros((tall, KEY_HEAD_SIZE), jnp.float32)], 0)
+        for n in range(row):
+            sweep = onward(sweep, n) + jnp.concatenate([blank, added(n)], 0)
+        whole = sweep[:KEY_HEAD_SIZE]
+        top = half(whole)
+        rest = half(whole - top.astype(jnp.float32))
+        sides = jnp.concatenate([top, rest], 1)
+        hop.wait_recv()
+        came = hop_in[...]
+        entry[...] = came
+        came_top = half(came)
+        came_rest = half(came - came_top.astype(jnp.float32))
+        both = mm(jnp.concatenate([came_top, came_rest], 0), sides)
+        hop_out[...] = (
+            both[:tall, :KEY_HEAD_SIZE]
+            + both[:tall, KEY_HEAD_SIZE:]
+            + both[tall:, :KEY_HEAD_SIZE]
+            + sweep[KEY_HEAD_SIZE:]
+        )
+
+        @pl.when(line < lines - 1)
+        def _():
+            hop.start()
+
+    state = entry[...]
+    before[0] = half(state)
+    for n in range(row - 1):
+        state = onward(state, n) + added(n)
+        before[n + 1] = half(state)
+
+    @pl.when(line == 0)
+    def _():
+        hop_out[...] = onward(state, row - 1) + added(row - 1)
+
+        @pl.when(line < lines - 1)
+        def _():
+            hop.start()
 
     returning = [
         pltpu.make_async_remote_copy(
@@ -317,31 +349,50 @@
 
     def term(where):
         columns = pl.ds(pl.multiple_of(where * wide, wide), wide)
-        return half(mm(normed, w_ref[:, columns]))
-
-    leaving = []
-    for off in range(1, groups):
-        terms[off] = term(peer(off))
-        copy = pltpu.make_async_remote_copy(
-            src_ref=terms.at[off],
-            dst_ref=landed.at[off],
-            send_sem=term_send.at[off],
-            recv_sem=term_recv.at[off],
-            device_id={"head": peer(off)},
+        return mm(normed, w_ref[:, columns])
+
+    chips = groups // 2
+    core = lax.rem(group, 2)
+    chip = group // 2
+
+    def other(off):
+        return 2 * lax.rem(chip + off, chips)
+
+    def term_copy(slot, where):
+        return pltpu.make_async_remote_copy(
+            src_ref=terms.at[slot],
+            dst_ref=landed.at[slot],
+            send_sem=term_send.at[slot],
+            recv_sem=term_recv.at[slot],
+            device_id={"head": where},
             device_id_type=mesh_id,
         )
+
+    order = [*range(1, chips), 0]
+    near = {}
+    for off in order:
+        terms[off] = half(term(other(off) + 1 - core))
+        near[off] = term_copy(off, 2 * chip + 1 - core)
+        near[off].start()
+    mine = {off: term(other(off) + core) for off in order}
+    far = []
+    for off in order[:-1]:
+        near[off].wait()
+        terms[chips + off] = half(mine[off] + landed[off].astype(jnp.float32))
+        copy = term_copy(chips + off, other(off) + core)
         copy.start()
-        leaving.append(copy)
-    total = term(group).astype(jnp.float32)
+        far.append((chips + off, copy))
     for h in range(heads):
         turned = jnp.concatenate([states[h * cut + c] for c in range(cut)], 0)
         check_ref[h] = (
             mm(maps_ref[h, :, :KEY_HEAD_SIZE], turned, ((1,), (1,)))
             + maps_ref[h, :, KEY_HEAD_SIZE:]
         )
-    for off, copy in enumerate(leaving, 1):
+    near[0].wait()
+    total = mine[0] + landed[0].astype(jnp.float32)
+    for slot, copy in far:
         copy.wait()
-        total = total + landed[off].astype(jnp.float32)
+        total = total + landed[slot].astype(jnp.float32)
     mixed_ref[...] = half(total)
 
     @pl.when(line < lines - 1)
@@ -392,6 +443,7 @@
             pltpu.VMEM((unit_count, tall, KEY_HEAD_SIZE), bf16),
             pltpu.VMEM((tall, KEY_HEAD_SIZE), f32),
             pltpu.VMEM((tall, KEY_HEAD_SIZE), f32),
+            pltpu.VMEM((tall, KEY_HEAD_SIZE), f32),
             pltpu.VMEM((groups, tokens, wide), bf16),
             pltpu.VMEM((groups, tokens, wide), bf16),
             dma((3,)),
@@ -407,7 +459,7 @@
             dma((groups,)),
         ],
         compiler_params=pltpu.CompilerParams(
-            collective_id=0, has_side_effects=True, vmem_limit_bytes=40 * 2**20
+            collective_id=0, has_side_effects=True, vmem_limit_bytes=63 * 2**20
         ),
     )(
         pre_qk, pre_value, taps_qk, taps_value, history, gates, rows, state_in, gain,

time: 68 us -> 67.6 us (level)
  local copies, waits for them, and re-layouts: 8.73 us -> 6.18 us
  other arithmetic: 0.1 us -> 1.29 us
  matrix products: 3.21 us -> 3.91 us
    unnamed x37 -> x23, local copies, waits for them, and re-layouts: 8.71 us -> 6.17 us
where the time goes in v5:
time: 67.6 us; the launch traced here: 67.4 us
  Pallas kernels  55.3 us (82%)
  local copies, waits for them, and re-layouts  6.18 us (9%)
  matrix products  3.91 us (6%)
  other arithmetic  1.29 us (2%)
  between operations  0.71 us (1%)
    pallas_call x1, Pallas kernels, layer(): pl.pallas_call(functools.partial(layer_kernel, count=count, groups=groups...  55.3 us
    unnamed x23, local copies, waits for them, and re-layouts  6.17 us
    dot_general x1, matrix products, local(): jnp.dot(hidden_in, w_value, preferred_element_type=jnp.float32)  1.45 us
    dot_general x1, matrix products, local(): jnp.dot(hidden_in, qk_flat, preferred_element_type=jnp.float32)  1.41 us

profile of v5, /device:TPU:7, one launch (start us, length us, event | category | flops | bytes accessed | tf_op | source)
XLA Modules:
  0.0 67.4 jit_solution(14873493342685221828)
XLA Ops:
  0.6 0.0 copy-start
  0.6 2.1 %copy.19 = bf16[256,8,2,256]{3,1,2,0:T(8,128)(2,1)S(1)} copy(bf16[256,8,2,256]{3,2,1,0:T(2,128)(2,1)} %bitcast.21) | data formatting | bytes 4194304
  2.8 0.0 copy-start.8
  2.8 0.0 copy-done
  2.8 1.4 %convolution_convert_fusion.1.pre_qk = bf16[256,512]{1,0:T(8,128)(2,1)} fusion(bf16[256,2048]{1,0:T(8,128)(2,1)S(1)} %copy-done, bf16[2048,512]{1,0:T(8,128)(2,1)S(1)} %bitcast.22), kind=kOutput, calls=%fused_computation.1 | convolution fusion | flops 537001984 | bytes 3407872 | tf_op jit(solution)/shard_map/dot_general | solution.py:492
  4.2 0.2 copy-done.8
  4.4 0.0 copy-start.3
  4.4 0.0 copy-start.4
  4.4 0.0 copy-start.2
  4.4 0.0 copy-start.1
  4.4 0.0 copy-start.5
  4.4 0.0 copy-start.6
  4.4 0.0 copy-start.7
  4.4 1.5 %convolution_convert_fusion.pre_value = bf16[256,512]{1,0:T(8,128)(2,1)} fusion(bf16[256,2048]{1,0:T(8,128)(2,1)S(1)} %copy-done, bf16[2048,512]{1,0:T(8,128)(2,1)S(1)} %copy-done.8), kind=kOutput, calls=%fused_computation | convolution fusion | flops 537001984 | bytes 3407872 | tf_op jit(solution)/shard_map/dot_general | solution.py:493
  5.9 0.0 copy-done.3
  5.9 0.6 copy.20
  6.5 0.0 copy-done.4
  6.5 0.0 copy-done.2
  6.5 0.6 fusion.4.history
  7.1 0.0 copy-done.1
  7.1 1.1 %fusion.gates_ref = bf16[256,128]{1,0:T(8,128)(2,1)} fusion(bf16[256,2048]{1,0:T(8,128)(2,1)S(1)} %copy-done, bf16[2048,8]{0,1:T(8,128)(2,1)S(1)} %reshape.22), kind=kOutput, calls=%fused_computation.3 | convolution fusion | flops 134250496 | bytes 1146880 | tf_op jit(solution)/shard_map/dot_general | solution.py:495
  8.2 0.0 copy-done.5
  8.2 0.0 copy-done.6
  8.2 0.0 copy-done.7
  8.2 0.1 fusion.5
  8.3 0.6 pad_maximum_fusion.rows_ref
  8.9 55.3 %shard_map.158 = (bf16[256,256]{1,0:T(8,128)(2,1)}, f32[4,128,128]{2,1,0:T(8,128)}) custom-call(bf16[256,512]{1,0:T(8,128)(2,1)} %convolution_convert_fusion.1.pre_qk, bf16[256,512]{1,0:T(8,128)(2,1)} %convolution_convert_fusion.pre_value, bf16[4,512]{1,0:T(4,128)(2,1)} %bitcast.25, bf16[4,512]{1,0:T(4,128)(2,1)} %taps_value.1, ...), custom_call_target="tpu_custom_call" | custom-call | tf_op jit(solution)/shard_map/pallas_call | solution.py:421
  64.2 1.6 %copy.24 = bf16[256,256]{1,0:T(8,128)(2,1)} copy(bf16[256,256]{1,0:T(8,128)(2,1)} %get-tuple-element.10) | data formatting | bytes 262144
  65.7 1.7 %copy.25 = f32[1,4,128,128]{3,2,1,0:T(8,128)} copy(f32[1,4,128,128]{3,2,1,0:T(8,128)} %bitcast.23) | data formatting | bytes 524288
  (3 shorter events, 0.0 us)
Async XLA Ops:
  0.6 2.2 %copy-start = (bf16[256,2048]{1,0:T(8,128)(2,1)S(1)}, bf16[256,2048]{1,0:T(8,128)(2,1)}, u32[]{:S(2)}) copy-start(bf16[256,2048]{1,0:T(8,128)(2,1)} %hidden_hbm.1) | copy-start | bytes 3145732
  2.8 1.6 %copy-start.8 = (bf16[2048,512]{1,0:T(8,128)(2,1)S(1)}, bf16[2048,512]{1,0:T(8,128)(2,1)}, u32[]{:S(2)}) copy-start(bf16[2048,512]{1,0:T(8,128)(2,1)} %param.17) | copy-start | bytes 6291460
  4.4 1.5 %copy-start.3 = (bf16[4,2,256]{2,1,0:T(2,128)(2,1)S(1)}, bf16[4,2,256]{2,1,0:T(2,128)(2,1)}, u32[]{:S(2)}) copy-start(bf16[4,2,256]{2,1,0:T(2,128)(2,1)} %param.20) | copy-start | bytes 12292
  4.4 2.1 %copy-start.4 = (bf16[3,2,256]{2,1,0:T(2,128)(2,1)S(1)}, bf16[3,2,256]{2,1,0:T(2,128)(2,1)}, u32[]{:S(2)}) copy-start(bf16[3,2,256]{2,1,0:T(2,128)(2,1)} %param.22) | copy-start | bytes 9220
  4.4 2.1 %copy-start.2 = (bf16[3,512]{1,0:T(4,128)(2,1)S(1)}, bf16[3,512]{1,0:T(4,128)(2,1)}, u32[]{:S(2)}) copy-start(bf16[3,512]{1,0:T(4,128)(2,1)} %param.23) | copy-start | bytes 9220
  4.4 2.7 %copy-start.1 = (bf16[2048,2,4]{0,2,1:T(4,128)(2,1)S(1)}, bf16[2048,2,4]{0,2,1:T(4,128)(2,1)}, u32[]{:S(2)}) copy-start(bf16[2048,2,4]{0,2,1:T(4,128)(2,1)} %param.19) | copy-start | bytes 98308
  4.4 3.8 %copy-start.5 = (f32[4]{0:T(128)S(1)}, f32[4]{0:T(128)}, u32[]{:S(2)}) copy-start(f32[4]{0:T(128)} %param.25) | copy-start | bytes 52
  4.4 3.8 %copy-start.6 = (f32[4]{0:T(128)S(1)}, f32[4]{0:T(128)}, u32[]{:S(2)}) copy-start(f32[4]{0:T(128)} %param.26) | copy-start | bytes 52
  4.4 3.8 %copy-start.7 = (f32[4]{0:T(128)S(1)}, f32[4]{0:T(128)}, u32[]{:S(2)}) copy-start(f32[4]{0:T(128)} %param.24) | copy-start | bytes 52
